TPU v7x, 32 devices: a whole 2x2x4 slice. The times are simulated.
32 devices in a mesh: grp: 2 (over y), hh: 4 (over z), per: 2 (over x), st: 2 (over core).
Axes of the slice: x: 2, y: 2, z: 4, core: 2. Of those that a mesh axis runs over, the one named last changes fastest.
Arguments:
- earnings: float32 [3072, 16], P(('hh', 'per')), may hold values from -5.4 to 5.4
- starts: int32 [3072], P(('hh', 'per')), may hold values from 0 to 12, as said below
- lengths: int32 [3072], P(('hh', 'per')), may hold values from 4 to 16
- block_count: int32 [8], P(('hh', 'per')), may hold values from 0 to 3, as said below
- trans_logits: bfloat16 [32, 256, 256], P(('grp', 'per', 'st')), parts along dimension 0, may hold values from -4 to 4
- init_logits: float32 [512], P('grp'), parts along dimension 0, may hold values from -4 to 4
- state_mean: float32 [512], P('grp'), parts along dimension 0, may hold values from -4 to 4
- log_sd: float32 [512], P('grp'), parts along dimension 0, may hold values from 0 to 1
Outputs:
- trans_grad: float32 [32, 256, 256], P(('grp', 'per'), 'hh', 'st'), parts along dimension 0
- mean_loglik: float32 [2], P('grp'), parts along dimension 0
There are 2 independent parts, one for each index of `grp`. A program takes and returns all parts, laid end to end along the dimension named above; an argument that names none is the same for every part. Nothing has to cross between parts.
Inputs may be any that keep to these rules, and one draw needn't show every extreme that they name: starts[h] + lengths[h] <= 16. Exactly 1 device hold 3 blocks and as many hold 2; the counts sum to 8. Only the first block_count[d] blocks of device d's 3 slots hold households; the entries of the other slots are to be ignored.
All inputs are finite; a program needn't handle non-finite values.
Results may differ from a plain program's by a relative error of at most 0.00055.
Values may be sent and summed in bfloat16 or wider, within the bound.
A program may use at most 64 MiB of HBM per device.

v0:
```python
import jax
import jax.numpy as jnp
from jax import lax
from jax.sharding import PartitionSpec as P

HB = 128


top_precision = lax.Precision.HIGHEST


def emission(column, state_mean, log_sd):
    z_score = (column[:, None] - state_mean[None, :]) / jnp.exp(log_sd)[None, :]
    return jnp.exp(-0.5 * z_score * z_score - log_sd[None, :])


def per_device(
    earnings, starts, lengths, block_count, trans_logits, init_logits, state_mean, log_sd
):
    num_states = init_logits.shape[0]
    num_periods = earnings.shape[1]
    slot_rows = earnings.shape[0]
    group_size = lax.axis_size(("hh", "per"))
    core_count = lax.axis_size("st")
    half_states = num_states // core_count
    lead_state = lax.axis_index("st") * half_states
    whole_logits = lax.all_gather(trans_logits, ("per", "st"), axis=0, tiled=True)
    raised = jnp.exp(whole_logits.astype(jnp.float32))
    trans_probs = raised / jnp.sum(raised, axis=2, keepdims=True)
    raised_first = jnp.exp(init_logits)
    first_probs = raised_first / jnp.sum(raised_first)
    source_rows = slot_rows // group_size
    count_out = jnp.broadcast_to(block_count.reshape(1, 1), (1, group_size))
    got_earn, got_start, got_len, got_count = (
        lax.all_to_all(
            earnings.reshape(source_rows, group_size, num_periods),
            ("hh", "per"),
            split_axis=1,
            concat_axis=1,
            tiled=True,
        ),
        lax.all_to_all(
            starts.reshape(source_rows, group_size),
            ("hh", "per"),
            split_axis=1,
            concat_axis=1,
            tiled=True,
        ),
        lax.all_to_all(
            lengths.reshape(source_rows, group_size),
            ("hh", "per"),
            split_axis=1,
            concat_axis=1,
            tiled=True,
        ),
        lax.all_to_all(count_out, ("hh", "per"), split_axis=1, concat_axis=1, tiled=True),
    )
    per_source = got_count[0] * (HB // group_size)
    ends_at = jnp.cumsum(per_source)
    target_ids = jnp.arange(HB, dtype=jnp.int32)
    before_mask = ends_at[None, :] <= target_ids[:, None]
    source_ids = jnp.sum(before_mask.astype(jnp.int32), axis=1)
    begins_at = jnp.sum(jnp.where(before_mask, per_source[None, :], 0), axis=1)
    pick_ids = (target_ids - begins_at) * group_size + source_ids
    rows_earn = jnp.take(got_earn.reshape(source_rows * group_size, num_periods), pick_ids, axis=0)
    rows_start = jnp.take(got_start.reshape(source_rows * group_size), pick_ids)
    rows_len = jnp.take(got_len.reshape(source_rows * group_size), pick_ids)
    row_live = jnp.ones((HB,), dtype=bool)
    years_local = jnp.sum(jnp.where(row_live, rows_len, 0)).astype(jnp.float32)
    row_total_count = rows_earn.shape[0]
    columns = rows_earn.T
    period_ids = jnp.arange(num_periods, dtype=jnp.int32)

    def observed(step_now):
        return row_live & (step_now >= rows_start) & (step_now < rows_start + rows_len)

    def forward(prev_alpha, inputs):
        matrix, column, step_now = inputs
        fresh_start = (step_now <= rows_start)[:, None]
        moved_mass = jnp.dot(
            prev_alpha, matrix, precision=top_precision, preferred_element_type=jnp.float32
        )
        joint_mass = jnp.where(fresh_start, first_probs[None, :], moved_mass) * emission(
            column, state_mean, log_sd
        )
        seen_now = observed(step_now)
        scale_now = jnp.where(seen_now, jnp.sum(joint_mass, axis=1), 1.0)
        new_alpha = jnp.where(seen_now[:, None], joint_mass / scale_now[:, None], prev_alpha)
        return (new_alpha, (new_alpha, scale_now))

    start_alpha = jnp.broadcast_to(first_probs[None, :], (row_total_count, num_states))
    _, (alphas, scales) = lax.scan(forward, start_alpha, (trans_probs, columns, period_ids))

    def carry_of(back_now, column, scale_now, step_now):
        seen_now = observed(step_now)
        return jnp.where(
            seen_now[:, None],
            emission(column, state_mean, log_sd) * back_now / scale_now[:, None],
            0.0,
        )

    def backward(carry_now, inputs):
        matrix, alpha_prev, column_prev, scale_prev, step_now = inputs
        moving = row_live & (step_now > rows_start) & (step_now < rows_start + rows_len)
        weights = jnp.where(moving[:, None], alpha_prev, 0.0)
        own_carry = lax.dynamic_slice_in_dim(carry_now, lead_state, half_states, 1)
        grad_term = lax.dot_general(
            weights,
            own_carry,
            (((0,), (0,)), ((), ())),
            precision=top_precision,
            preferred_element_type=jnp.float32,
        )
        pulled = lax.dot_general(
            carry_now,
            matrix,
            (((1,), (1,)), ((), ())),
            precision=top_precision,
            preferred_element_type=jnp.float32,
        )
        back_now = jnp.where(moving[:, None], pulled, 1.0)
        return (carry_of(back_now, column_prev, scale_prev, step_now - 1), grad_term)

    ones_back = jnp.ones((row_total_count, num_states), jnp.float32)
    last_carry = carry_of(
        ones_back, columns[num_periods - 1], scales[num_periods - 1], num_periods - 1
    )
    _, grad_terms = lax.scan(
        backward,
        last_carry,
        (trans_probs[1:], alphas[:-1], columns[:-1], scales[:-1], period_ids[1:]),
        reverse=True,
    )
    zero_first = jnp.zeros((1,) + grad_terms.shape[1:], jnp.float32)
    partial_counts = jnp.concatenate([zero_first, grad_terms], axis=0)
    loglik_local = jnp.sum(jnp.log(scales))
    summed = lax.psum_scatter(partial_counts, "hh", scatter_dimension=1, tiled=True)
    summed = lax.psum_scatter(summed, "per", scatter_dimension=0, tiled=True)
    loglik_share = loglik_local / core_count
    years_share = years_local / core_count
    period_block = summed.shape[0]
    row_block_size = summed.shape[1]
    local_probs = lax.dynamic_slice(
        trans_probs,
        (lax.axis_index("per") * period_block, lax.axis_index("hh") * row_block_size, lead_state),
        (period_block, row_block_size, half_states),
    )
    weighted = local_probs * summed
    row_total, loglik_core, years_core = lax.psum(
        (jnp.sum(weighted, axis=2), loglik_share, years_share), "st"
    )
    loglik_all, years_all = lax.psum((loglik_core, years_core), ("hh", "per"))
    factor = float(num_states * num_states * num_periods) / years_all
    trans_grad = factor * (weighted - local_probs * row_total[:, :, None])
    mean_loglik = jnp.reshape(loglik_all / years_all, (1,))
    return (trans_grad, mean_loglik)


def solution(mesh):
    placed = (
        P(("hh", "per"), None),
        P(("hh", "per")),
        P(("hh", "per")),
        P(("hh", "per")),
        P(("grp", "per", "st"), None, None),
        P("grp"),
        P("grp"),
        P("grp"),
    )
    return jax.shard_map(
        per_device,
        mesh=mesh,
        in_specs=placed,
        out_specs=(P(("grp", "per"), "hh", "st"), P("grp")),
        check_vma=False,
    )
```

profile of v0, /device:TPU:0, one launch (start us, length us, event | category | flops | bytes accessed | tf_op | source)
XLA Modules:
  0.0 298.8 jit_solution(5646740172056218741)
XLA Ops:
  9.1 7.3 %all-to-all-start.1 = ((s32[1,8,1]{2,0,1:T(1,128)}), s32[1,8,1]{2,0,1:T(1,128)S(1)}, u32[]{:S(2)}, u32[]{:S(2)}) async-start(s32[1,8,1]{2,0,1:T(1,128)} %broadcast_in_dim.209), calls=%async_computation.1 | async-start | bytes 8192 | tf_op jit(solution)/shard_map/all_to_all | solution.py:56
  24.3 6.0 %all-to-all-start = ((s32[48,8,1]{0,2,1:T(1,128)}), s32[48,8,1]{0,2,1:T(1,128)S(1)}, u32[]{:S(2)}, u32[]{:S(2)}) async-start(s32[48,8,1]{0,2,1:T(1,128)} %copy.34), calls=%async_computation | async-start | bytes 8192 | tf_op jit(solution)/shard_map/all_to_all | solution.py:49
  30.8 5.9 %all-to-all-done = s32[48,8,1]{0,2,1:T(1,128)S(1)} async-done(((s32[48,8,1]{0,2,1:T(1,128)}), s32[48,8,1]{0,2,1:T(1,128)S(1)}, u32[]{:S(2)}, u32[]{:S(2)}) %all-to-all-start) | async-done | bytes 1568 | tf_op jit(solution)/shard_map/all_to_all | solution.py:49
  36.8 3.3 %all-to-all-start.2 = ((s32[48,8,1]{0,2,1:T(1,128)}), s32[48,8,1]{0,2,1:T(1,128)S(1)}, u32[]{:S(2)}, u32[]{:S(2)}) async-start(s32[48,8,1]{0,2,1:T(1,128)} %copy.36), calls=%async_computation.2 | async-start | bytes 8192 | tf_op jit(solution)/shard_map/all_to_all | solution.py:42
  40.2 6.2 %all-to-all-done.2 = s32[48,8,1]{0,2,1:T(1,128)S(1)} async-done(((s32[48,8,1]{0,2,1:T(1,128)}), s32[48,8,1]{0,2,1:T(1,128)S(1)}, u32[]{:S(2)}, u32[]{:S(2)}) %all-to-all-start.2) | async-done | bytes 1568 | tf_op jit(solution)/shard_map/all_to_all | solution.py:42
  46.5 3.3 %all-to-all-start.3 = ((f32[8,1,768]{2,1,0:T(1,128)}), f32[8,1,768]{2,1,0:T(1,128)S(1)}, u32[]{:S(2)}, u32[]{:S(2)}) async-start(f32[8,1,768]{2,1,0:T(1,128)} %reshape.291), calls=%async_computation.3 | async-start | bytes 49152 | tf_op jit(solution)/shard_map/all_to_all | solution.py:35
  52.6 3.8 %all-to-all-done.3 = f32[8,1,768]{2,1,0:T(1,128)S(1)} async-done(((f32[8,1,768]{2,1,0:T(1,128)}), f32[8,1,768]{2,1,0:T(1,128)S(1)}, u32[]{:S(2)}, u32[]{:S(2)}) %all-to-all-start.3) | async-done | bytes 24608 | tf_op jit(solution)/shard_map/all_to_all | solution.py:35
  58.9 2.4 fusion.28
  62.2 2.3 slice.36
  65.4 68.4 %while.34 = (s32[]{:T(128)}, f32[128,256]{0,1:T(8,128)S(1)}, f32[16,128,256]{1,2,0:T(8,128)S(1)}, f32[16,128]{1,0:T(8,128)S(1)}, s32[16]{0:T(128)S(1)}, /*index=...) while((s32[]{:T(128)}, f32[128,256]{0,1:T(8,128)S(1)}, ...), condition=%wide.region_10.12_spmd, body=%wide.region_8.11_spmd.sunk | while | flops 100992000 | bytes 1062457 | solution.py:92
  66.7 1.6 fusion.54
  71.0 1.6 fusion.54
  75.3 1.6 fusion.54
  79.5 1.6 fusion.54
  83.8 1.6 fusion.54
  88.1 1.6 fusion.54
  92.4 1.6 fusion.54
  96.6 1.6 fusion.54
  100.9 1.6 fusion.54
  105.2 1.6 fusion.54
  109.5 1.6 fusion.54
  113.8 1.6 fusion.54
  118.0 1.6 fusion.54
  122.3 1.6 fusion.54
  126.6 1.6 fusion.54
  130.9 1.6 fusion.54
  133.9 1.5 slice.27
  135.7 67.4 %while.35 = (s32[]{:T(128)}, f32[128,256]{0,1:T(8,128)S(1)}, f32[15,256,128]{2,1,0:T(8,128)S(1)}, s32[15]{0:T(128)S(1)}, s32[128]{0:T(128)S(1)}, /*index=5*/s32[...) while((s32[]{:T(128)}, f32[128,256]{0,1:T(8,128)S(1)}, ...), condition=%wide.region_12.14_spmd, body=%wide.region_11.13_spmd.sunk | while | flops 151323392 | bytes 1124049 | solution.py:128
  138.9 1.3 fusion.60
  143.4 1.3 fusion.60
  147.9 1.3 fusion.60
  152.4 1.3 fusion.60
  156.9 1.3 fusion.60
  161.3 1.3 fusion.60
  165.8 1.3 fusion.60
  170.3 1.3 fusion.60
  174.8 1.3 fusion.60
  179.3 1.3 fusion.60
  183.8 1.3 fusion.60
  188.3 1.3 fusion.60
  197.3 1.3 fusion.60
  201.8 1.3 fusion.60
  203.1 1.6 concatenate.3
  204.8 41.3 %reduce-scatter.3.cloned.1.call-done = f32[16,64,128]{2,1,0:T(8,128)} async-done(((f32[16,256,128]{2,1,0:T(8,128)}), f32[16,64,128]{2,1,0:T(8,128)}) %reduce-scatter.3.cloned.1.call-update) | async-done | bytes 524304 | tf_op jit(solution)/shard_map/reduce_scatter | solution.py:137
  248.6 13.5 %reduce-scatter.5.cloned.1.call-done = f32[8,64,128]{2,1,0:T(8,128)} async-done(((f32[16,64,128]{2,1,0:T(8,128)}), f32[8,64,128]{2,1,0:T(8,128)}) %reduce-scatter.5.cloned.1.call-update) | async-done | bytes 262160 | tf_op jit(solution)/shard_map/reduce_scatter | solution.py:138
  263.4 3.0 %all-reduce.2 = (f32[8,64]{1,0:T(8,128)S(1)}, f32[]{:T(128)}, f32[]{:T(128)}) all-reduce(f32[8,64]{1,0:T(8,128)S(1)} %fusion.33, f32[]{:T(128)S(6)} %div.140, f32[]{:T(128)S(6)} %div.151), channel_id=1, replica_groups=mesh['grp'=2,'hh'=4,'per'=2,'st'=2] {'st'}, use_global_device_ids=true, to_apply=%region_16.18 | all-reduce | flops 514 | bytes 4112 | tf_op jit(solution)/shard_map/psum | solution.py:149
  266.4 21.0 %all-reduce.1 = (f32[]{:T(128)}, f32[]{:T(128)}) all-reduce(f32[]{:T(128)} %get-tuple-element.712, f32[]{:T(128)} %get-tuple-element.713), channel_id=1, replica_groups=mesh['grp'=2,'hh'=4,'per'=2,'st'=2] {'hh','per'}, use_global_device_ids=true, to_apply=%region_5.7 | all-reduce | flops 2 | bytes 16 | tf_op jit(solution)/shard_map/psum | solution.py:152
  289.3 1.9 subtract_multiply_fusion
  (251 shorter events, 99.8 us)
Async XLA Ops:
  7.2 51.7 %all-gather.2.cloned.1.call-start = ((), (), s32[]{:S(2)}) async-start(), calls=%async_computation.6 | async-start | bytes 2621440 | tf_op jit(solution)/shard_map/all_gather | solution.py:27
  9.1 15.1 %all-to-all-start.1 = ((s32[1,8,1]{2,0,1:T(1,128)}), s32[1,8,1]{2,0,1:T(1,128)S(1)}, u32[]{:S(2)}, u32[]{:S(2)}) async-start(s32[1,8,1]{2,0,1:T(1,128)} %broadcast_in_dim.209), calls=%async_computation.1 | async-start | bytes 8192 | tf_op jit(solution)/shard_map/all_to_all | solution.py:56
  24.3 12.5 %all-to-all-start = ((s32[48,8,1]{0,2,1:T(1,128)}), s32[48,8,1]{0,2,1:T(1,128)S(1)}, u32[]{:S(2)}, u32[]{:S(2)}) async-start(s32[48,8,1]{0,2,1:T(1,128)} %copy.34), calls=%async_computation | async-start | bytes 8192 | tf_op jit(solution)/shard_map/all_to_all | solution.py:49
  36.8 9.7 %all-to-all-start.2 = ((s32[48,8,1]{0,2,1:T(1,128)}), s32[48,8,1]{0,2,1:T(1,128)S(1)}, u32[]{:S(2)}, u32[]{:S(2)}) async-start(s32[48,8,1]{0,2,1:T(1,128)} %copy.36), calls=%async_computation.2 | async-start | bytes 8192 | tf_op jit(solution)/shard_map/all_to_all | solution.py:42
  46.5 9.9 %all-to-all-start.3 = ((f32[8,1,768]{2,1,0:T(1,128)}), f32[8,1,768]{2,1,0:T(1,128)S(1)}, u32[]{:S(2)}, u32[]{:S(2)}) async-start(f32[8,1,768]{2,1,0:T(1,128)} %reshape.291), calls=%async_computation.3 | async-start | bytes 49152 | tf_op jit(solution)/shard_map/all_to_all | solution.py:35
  49.8 196.3 %reduce-scatter.3.cloned.1.call-start = ((), (), s32[]{:S(2)}) async-start(), calls=%async_computation.7 | async-start | bytes 2621440 | tf_op jit(solution)/shard_map/reduce_scatter | solution.py:137
  58.9 2.4 copy-start.1
  62.2 3.1 %copy-start = (f32[16,256,256]{2,1,0:T(8,128)}, f32[16,256,256]{2,1,0:T(8,128)S(1)}, u32[]{:S(2)}) copy-start(f32[16,256,256]{2,1,0:T(8,128)S(1)} %fusion.27) | copy-start | bytes 12582916
  62.2 3.2 %copy-start.2 = (f32[256]{0:T(256)S(1)}, f32[256]{0:T(256)}, u32[]{:S(2)}) copy-start(f32[256]{0:T(256)} %param.21) | copy-start | bytes 3076
  62.2 3.2 %copy-start.3 = (f32[256]{0:T(256)S(1)}, f32[256]{0:T(256)}, u32[]{:S(2)}) copy-start(f32[256]{0:T(256)} %param.20) | copy-start | bytes 3076
  204.7 57.5 %reduce-scatter.5.cloned.1.call-start = ((), (), s32[]{:S(2)}) async-start(), calls=%async_computation.8 | async-start | bytes 786432 | tf_op jit(solution)/shard_map/reduce_scatter | solution.py:138
Sparse Core Ops, SparseCore 0:
  9.5 25.2 all-gather.1
  204.8 41.1 reduce-scatter.2
  248.3 13.8 reduce-scatter.4
where the time goes:
time: 301 us; the launch traced here: 299 us
  waiting for transfers between devices  71.5 us (24%)
  matrix products  63.4 us (21%)
  other arithmetic  53.2 us (18%)
  local copies, waits for them, and re-layouts  36.2 us (12%)
  blocking collectives  24 us (8%)
  starting transfers between devices  20 us (7%)
  between operations  19 us (6%)
  loops' own time  11.4 us (4%)
    reduce_scatter x1, waiting for transfers between devices, per_device(): lax.psum_scatter(partial_counts, 'hh', scatter_dimension=1, tiled=True)  41.3 us
    dot_general x16, matrix products, forward(): jnp.dot(prev_alpha, matrix, precision=top_precision, preferred_element_ty...  25.6 us
    psum x1, blocking collectives, per_device(): loglik_all, years_all = lax.psum((loglik_core, years_core), ('hh', 'per'))  21 us
    select_n x32, other arithmetic, forward(): scale_now = jnp.where(seen_now, jnp.sum(joint_mass, axis=1), 1.0)  20.9 us
    dot_general x15, matrix products, backward(): lax.dot_general(carry_now, matrix, (((1,), (1,)), ((), ())), precision=to...  20 us
    dot_general x15, matrix products, backward(): lax.dot_general(weights, own_carry, (((0,), (0,)), ((), ())), precision=t...  17.8 us
    reduce_scatter x1, waiting for transfers between devices, per_device(): summed = lax.psum_scatter(summed, 'per', scatter_dimension=0, tiled=True)  13.5 us
    another operation x1, loops' own time, per_device(): lax.scan(backward, last_carry, (trans_probs[1:], alphas[:-1], columns[:-1...  10.6 us
  transfers between devices with their start and end apart: 7, of which 5 were waited for; matrix products, arithmetic and copies ran while one was open for 5% of the time, Pallas kernels for 0%

commit v1 on v0

--- a/solution.py
+++ b/solution.py
@@ -1,7 +1,11 @@
+import functools
+
 import jax
 import jax.numpy as jnp
 from jax import lax
 from jax.sharding import PartitionSpec as P
+from jax.experimental import pallas as pl
+from jax.experimental.pallas import tpu as pltpu
 
 HB = 128
 
@@ -156,7 +160,409 @@
     return (trans_grad, mean_loglik)
 
 
+F32 = jnp.float32
+BF = jnp.bfloat16
+MESH = pl.DeviceIdType.MESH
+
+
+def split_hi_lo(v):
+    hi = v.astype(BF)
+    return hi, (v - hi.astype(F32)).astype(BF)
+
+
+def dot3(a, hi, lo, dims):
+    ah, al = split_hi_lo(a)
+    dd = lambda p, q: lax.dot_general(p, q, (dims, ((), ())), preferred_element_type=F32)
+    return dd(ah, hi) + (dd(al, hi) + dd(ah, lo))
+
+
+def fused_kernel(cfg, pack, logits, par, out, llout,
+                 lg, got, amem, bmem, xsend, xrecv, aown, apart, uown, upart,
+                 cbuf, zrecv, llbox, rts, rtr,
+                 gsend, grecv, lrecv, lsend_p, lsend_x, lsend_r,
+                 xs_sem, xr_sem, as_sem, ar_sem, us_sem, ur_sem,
+                 zs_sem, zr_sem, lls_sem, llr_sem, rs_sem, rr_sem):
+    nz, nt, half_t, own_t, rows, num_states = cfg
+    x = lax.axis_index("per")
+    z = lax.axis_index("hh")
+    s = lax.axis_index("st")
+    half = num_states // 2
+    nsrc = nz * 2
+    zr = num_states // nz
+    slab = pack.shape[1]
+
+    def rcopy(src, dst, ss, rs, dev):
+        return pltpu.make_async_remote_copy(
+            src_ref=src, dst_ref=dst, send_sem=ss, recv_sem=rs,
+            device_id=dev, device_id_type=MESH)
+
+    def arrived(ref, sem):
+        pltpu.make_async_copy(ref, ref, sem).wait()
+
+    barrier = pltpu.get_barrier_semaphore()
+    others = []
+    for dz in range(nz):
+        for dx in range(2):
+            for ds in range(2):
+                if dz or dx or ds:
+                    others.append({"hh": lax.rem(z + dz, nz), "per": lax.rem(x + dx, 2), "st": lax.rem(s + ds, 2)})
+    for dev in others:
+        pl.semaphore_signal(barrier, inc=1, device_id=dev, device_id_type=MESH)
+    pl.semaphore_wait(barrier, len(others))
+
+    partner = {"hh": z, "per": x, "st": 1 - s}
+    across = {"hh": z, "per": 1 - x, "st": s}
+
+    me_src = z * 2 + x
+    hist = []
+    n = 0
+    for dz in range(nz):
+        for dx in range(2):
+            tz, tx = lax.rem(z + dz, nz), lax.rem(x + dx, 2)
+            if dz == 0 and dx == 0:
+                c = pltpu.make_async_copy(pack.at[tz * 2 + s], got.at[me_src], grecv.at[0])
+            else:
+                c = rcopy(pack.at[tz * 2 + s], got.at[me_src], gsend.at[n], grecv.at[n],
+                          {"hh": tz, "per": tx, "st": s})
+            c.start()
+            hist.append(c)
+            n += 1
+
+    mine = own_t * (2 * x + s)
+    sends = []
+    for i in range(own_t):
+        off = jnp.where(x == 0, own_t - 1 - i, i)
+        near = own_t - 1 - off
+        p = mine + near
+        c = rcopy(logits.at[near], lg.at[p], lsend_p.at[i], lrecv.at[p], partner)
+        c.start()
+        sends.append(c)
+        c = pltpu.make_async_copy(logits.at[near], lg.at[p], lrecv.at[p])
+        c.start()
+    for i in range(own_t):
+        off = jnp.where(x == 0, own_t - 1 - i, i)
+        p = mine + off
+        c = rcopy(logits.at[off], lg.at[p], lsend_x.at[i], lrecv.at[p], across)
+        c.start()
+        sends.append(c)
+
+    init = par[0:1, :]
+    mean = par[1:2, :]
+    log_sd = par[2:3, :]
+    raised_first = jnp.exp(init)
+    first = raised_first / jnp.sum(raised_first, axis=1, keepdims=True)
+    inv_sd = jnp.exp(-log_sd)
+
+    for n in range(nsrc):
+        if n == 0:
+            hist[0].wait()
+        else:
+            hist[n].wait_recv()
+    base = jnp.zeros((1, 1), F32)
+    years = jnp.zeros((1, 1), F32)
+    picked = jnp.zeros((rows, 128), F32)
+    lane = lax.broadcasted_iota(jnp.int32, (slab, rows), 1).astype(F32)
+    sub = lax.broadcasted_iota(jnp.int32, (slab, rows), 0).astype(F32)
+    for src in range(nsrc):
+        g = got[src]
+        live = g[0:1, nt + 2:nt + 3] * float(rows // nsrc)
+        years = years + g[0:1, nt + 3:nt + 4]
+        onehot = jnp.where((sub + base == lane) & (sub < live), 1.0, 0.0)
+        picked = picked + lax.dot_general(
+            onehot, g, (((0,), (0,)), ((), ())),
+            precision=lax.Precision.HIGHEST, preferred_element_type=F32)
+        base = base + live
+    start = picked[:, nt:nt + 1]
+    stop = start + picked[:, nt + 1:nt + 2]
+
+    def emit(t):
+        zs = (picked[:, t:t + 1] - mean) * inv_sd
+        return jnp.exp(-0.5 * zs * zs - log_sd)
+
+    def probs(t):
+        r = jnp.exp(lg[t].astype(F32))
+        return split_hi_lo(r / jnp.sum(r, axis=1, keepdims=True))
+
+    def halves(ref, k, v):
+        ref[k, 0] = v[:, :half]
+        ref[k, 1] = v[:, half:]
+
+    def whole(ref, k):
+        return jnp.concatenate([ref[k, 0], ref[k, 1]], axis=1)
+
+    def relay(i, xs):
+        q = own_t * (2 * (1 - xs) + s) + (i if xs == 0 else own_t - 1 - i)
+        arrived(lg.at[q], lrecv.at[q])
+        c = rcopy(lg.at[q], lg.at[q], lsend_r.at[i], lrecv.at[q], partner)
+        c.start()
+
+    def need(t, xs):
+        if (t // half_t) == xs:
+            arrived(lg.at[t], lrecv.at[t])
+        else:
+            @pl.when(t // own_t != 2 * (1 - xs) + s)
+            def _():
+                arrived(lg.at[t], lrecv.at[t])
+
+    def send_across(k, v):
+        halves(xsend, k, v.astype(BF))
+        rcopy(xsend.at[k], xrecv.at[k], xs_sem.at[k], xr_sem.at[k], across).start()
+
+    def moving(t):
+        return (float(t) > start) & (float(t) < stop)
+
+    def stage_one(k, xs):
+        arrived(xrecv.at[k], xr_sem.at[k])
+        q = xs * half_t + k
+        zsum = jnp.sum(whole(xrecv, k).astype(F32) * bmem[k], axis=1, keepdims=True)
+        weight = jnp.where(moving(q), 1.0 / jnp.where(moving(q), zsum, 1.0), 0.0)
+        scaled = (amem[k] * weight).astype(BF)
+        if xs == 0:
+            halves(aown, k, scaled)
+            rcopy(aown.at[k], apart.at[k], as_sem.at[k], ar_sem.at[k], partner).start()
+            rcopy(xrecv.at[k, 1 - s], upart.at[k], us_sem.at[k], ur_sem.at[k], partner).start()
+        else:
+            halves(uown, k, scaled)
+            rcopy(xrecv.at[k], apart.at[k], as_sem.at[k], ar_sem.at[k], partner).start()
+            rcopy(uown.at[k, 1 - s], upart.at[k], us_sem.at[k], ur_sem.at[k], partner).start()
+
+    def stage_two(k, xs):
+        arrived(apart.at[k], ar_sem.at[k])
+        arrived(upart.at[k], ur_sem.at[k])
+        a_ref, u_ref = (aown, xrecv) if xs == 0 else (xrecv, uown)
+        u_all = jnp.concatenate([u_ref[k, s], upart[k]], axis=0)
+        for b in range(2):
+            a_all = jnp.concatenate([a_ref[k, b], apart[k, b]], axis=0)
+            cbuf[k, b * half:(b + 1) * half, :] = lax.dot_general(
+                a_all, u_all, (((0,), (0,)), ((), ())), preferred_element_type=F32)
+        for dz in range(1, nz):
+            tz = lax.rem(z + dz, nz)
+            rcopy(cbuf.at[k, pl.ds(pl.multiple_of(tz * zr, 8), zr)], zrecv.at[dz - 1, k],
+                  zs_sem.at[dz - 1, k], zr_sem.at[dz - 1, k],
+                  {"hh": tz, "per": x, "st": s}).start()
+
+    relay_at = {2: 0, 4: 1, 6: 2, 8: 3}
+
+    @pl.when(x == 0)
+    def _forward():
+        todo = list(range(half_t - 1, 0, -1))
+        ready = []
+        total = jnp.zeros((rows, 1), F32)
+        joint = scale_inv = None
+        for t in range(nt):
+            if t in relay_at:
+                relay(relay_at[t], 0)
+            e = emit(t)
+            if t == 0:
+                need(0, 0)
+                joint = first * e
+            else:
+                need(t, 0)
+                hi, lo = probs(t)
+                moved = dot3(joint, hi, lo, ((1,), (0,))) * scale_inv
+                if t < half_t:
+                    bmem[t] = moved
+                joint = jnp.where(float(t) <= start, first, moved) * e
+            scale = jnp.sum(joint, axis=1, keepdims=True)
+            seen = (float(t) >= start) & (float(t) < stop)
+            total = total + jnp.where(seen, jnp.log(scale), 0.0)
+            scale_inv = 1.0 / scale
+            if t < half_t - 1:
+                amem[t + 1] = joint * scale_inv
+            elif t < nt - 1:
+                send_across(t - (half_t - 1), joint * scale_inv)
+            if t >= half_t + 1:
+                if ready:
+                    stage_two(ready.pop(0), 0)
+                if todo:
+                    k = todo.pop(0)
+                    stage_one(k, 0)
+                    ready.append(k)
+        llsum = jnp.sum(total, axis=0, keepdims=True)
+        llbox[z * 2 + s] = jnp.broadcast_to(llsum, (8, 128))
+        for j, dev in enumerate(others):
+            rcopy(llbox.at[z * 2 + s], llbox.at[z * 2 + s], lls_sem.at[j], llr_sem.at[z * 2 + s], dev).start()
+        while todo or ready:
+            if ready:
+                stage_two(ready.pop(0), 0)
+            if todo:
+                k = todo.pop(0)
+                stage_one(k, 0)
+                ready.append(k)
+        for j, dev in enumerate(others):
+            rcopy(llbox.at[z * 2 + s], llbox.at[z * 2 + s], lls_sem.at[j], llr_sem.at[z * 2 + s], dev).wait_send()
+
+    @pl.when(x == 1)
+    def _backward():
+        todo = list(range(half_t))
+        ready = []
+        back = jnp.ones((rows, num_states), F32)
+        for step in range(nt - 1):
+            t = nt - 1 - step
+            if step in relay_at:
+                relay(relay_at[step], 1)
+            need(t, 1)
+            hi, lo = probs(t)
+            v = emit(t) * back
+            norm_inv = 1.0 / jnp.sum(v, axis=1, keepdims=True)
+            mv = moving(t)
+            u = jnp.where(mv, v * norm_inv, 0.0)
+            if t >= half_t:
+                amem[t - half_t] = u
+            else:
+                send_across(t, u)
+            if t > 1:
+                back = jnp.where(mv, dot3(v, hi, lo, ((1,), (1,))) * norm_inv, 1.0)
+                if t >= half_t:
+                    bmem[t - half_t] = back
+            if step >= half_t + 1:
+                if ready:
+                    stage_two(ready.pop(0), 1)
+                if todo:
+                    k = todo.pop(0)
+                    stage_one(k, 1)
+                    ready.append(k)
+        need(0, 1)
+        while todo or ready:
+            if ready:
+                stage_two(ready.pop(0), 1)
+            if todo:
+                k = todo.pop(0)
+                stage_one(k, 1)
+                ready.append(k)
+
+    zrow = pl.ds(pl.multiple_of(z * zr, 8), zr)
+    col = pl.ds(pl.multiple_of(s * half, 128), half)
+    lane_out = lax.broadcasted_iota(jnp.int32, (zr, 128), 1)
+    sums = jnp.zeros((zr, 128), F32)
+
+    def slot(k, carry):
+        q = x * half_t + k
+
+        @pl.when(q > 0)
+        def _():
+            for d in range(nz - 1):
+                arrived(zrecv.at[d, k], zr_sem.at[d, k])
+            c = cbuf[k, zrow, :]
+            for d in range(nz - 1):
+                c = c + zrecv[d, k]
+            r = jnp.exp(lg[q, zrow, :].astype(F32))
+            mine_r = jnp.exp(lg[q, zrow, col].astype(F32))
+            bmem[k, 0:zr, 0:half] = mine_r / jnp.sum(r, axis=1, keepdims=True)
+            out[k] = bmem[k, 0:zr, 0:half] * c
+
+        @pl.when(q == 0)
+        def _():
+            bmem[k, 0:zr, 0:half] = jnp.zeros((zr, half), F32)
+            out[k] = jnp.zeros((zr, half), F32)
+        row = jnp.sum(out[k], axis=1, keepdims=True)
+        return carry + jnp.where(lane_out == k, row, 0.0)
+
+    sums = lax.fori_loop(0, half_t, slot, sums)
+    rts[...] = sums
+    rc = rcopy(rts, rtr, rs_sem.at[0], rr_sem.at[0], partner)
+    rc.start()
+
+    for src in range(nsrc):
+        @pl.when((x == 1) | (z * 2 + s != src))
+        def _():
+            arrived(llbox.at[src], llr_sem.at[src])
+    ll = llbox[0, 0:1, :]
+    for src in range(1, nsrc):
+        ll = ll + llbox[src, 0:1, :]
+    llout[...] = ll / years
+    factor = float(num_states * num_states * nt) / years
+    rc.wait()
+    rtot = rts[...] + rtr[...]
+    for k in range(half_t):
+        out[k] = factor * (out[k] - bmem[k, 0:zr, 0:half] * rtot[:, k:k + 1])
+
+    for n in range(1, nsrc):
+        hist[n].wait_send()
+    for c in sends:
+        c.wait_send()
+    for i in range(own_t):
+        rcopy(lg.at[0], lg.at[0], lsend_r.at[i], lrecv.at[0], partner).wait_send()
+    for k in range(half_t):
+        def drain(k=k):
+            rcopy(aown.at[k], apart.at[k], as_sem.at[k], ar_sem.at[k], partner).wait_send()
+            rcopy(uown.at[k, 0], upart.at[k], us_sem.at[k], ur_sem.at[k], partner).wait_send()
+            for d in range(nz - 1):
+                rcopy(cbuf.at[k, pl.ds(0, zr)], zrecv.at[d, k], zs_sem.at[d, k], zr_sem.at[d, k], partner).wait_send()
+        if k == 0:
+            pl.when(x == 1)(drain)
+            @pl.when(x == 0)
+            def _():
+                rcopy(xsend.at[0], xrecv.at[0], xs_sem.at[0], xr_sem.at[0], across).wait_send()
+        else:
+            drain()
+            rcopy(xsend.at[k], xrecv.at[k], xs_sem.at[k], xr_sem.at[k], across).wait_send()
+
+
+def fused_device(
+    earnings, starts, lengths, block_count, trans_logits, init_logits, state_mean, log_sd
+):
+    num_states = init_logits.shape[0]
+    nt = earnings.shape[1]
+    slot_rows = earnings.shape[0]
+    nz = lax.axis_size("hh")
+    nsrc = nz * 2
+    slab = slot_rows // nsrc
+    own_t = trans_logits.shape[0]
+    half_t = nt // 2
+    half = num_states // 2
+    zr = num_states // nz
+    rows = HB
+    count = block_count.astype(F32)[0]
+    live = jnp.arange(slot_rows, dtype=jnp.int32) < block_count[0] * HB
+    years = jnp.sum(jnp.where(live, lengths, 0)).astype(F32)
+    pack = jnp.concatenate(
+        [earnings, starts.astype(F32)[:, None], lengths.astype(F32)[:, None],
+         jnp.broadcast_to(count, (slot_rows, 1)), jnp.broadcast_to(years, (slot_rows, 1)),
+         jnp.zeros((slot_rows, 128 - nt - 4), F32)], axis=1)
+    pack = pack.reshape(slab, nsrc, 128).transpose(1, 0, 2)
+    par = jnp.concatenate(
+        [init_logits[None], state_mean[None], log_sd[None], jnp.zeros((5, num_states), F32)], axis=0)
+    cfg = (nz, nt, half_t, own_t, rows, num_states)
+    V = pltpu.VMEM
+    D = pltpu.SemaphoreType.DMA
+    vm = pl.BlockSpec(memory_space=pltpu.VMEM)
+    grad, ll = pl.pallas_call(
+        functools.partial(fused_kernel, cfg),
+        out_shape=(jax.ShapeDtypeStruct((half_t, zr, half), F32),
+                   jax.ShapeDtypeStruct((1, 128), F32)),
+        in_specs=[vm] * 3,
+        out_specs=(vm, vm),
+        scratch_shapes=[
+            V((nt, num_states, num_states), BF),
+            V((nsrc, slab, 128), F32),
+            V((half_t, rows, num_states), F32),
+            V((half_t, rows, num_states), F32),
+            V((half_t, 2, rows, half), BF),
+            V((half_t, 2, rows, half), BF),
+            V((half_t, 2, rows, half), BF),
+            V((half_t, 2, rows, half), BF),
+            V((half_t, 2, rows, half), BF),
+            V((half_t, rows, half), BF),
+            V((half_t, num_states, half), F32),
+            V((nz - 1, half_t, zr, half), F32),
+            V((nsrc, 8, 128), F32),
+            V((zr, 128), F32),
+            V((zr, 128), F32),
+            D((nsrc,)), D((nsrc,)), D((nt,)), D((own_t,)), D((own_t,)), D((own_t,)),
+            D((half_t,)), D((half_t,)), D((half_t,)), D((half_t,)), D((half_t,)), D((half_t,)),
+            D((nz - 1, half_t)), D((nz - 1, half_t)), D((4 * nz,)), D((nsrc,)), D((1,)), D((1,)),
+        ],
+        compiler_params=pltpu.CompilerParams(
+            collective_id=0, has_side_effects=True, vmem_limit_bytes=56 * 1024 * 1024),
+        name="chain",
+    )(pack, trans_logits, par)
+    return grad, ll[0, 0:1]
+
+
 def solution(mesh):
+    fits = mesh.shape["per"] == 2 and mesh.shape["st"] == 2 and HB % (mesh.shape["hh"] * 2) == 0
+    body = fused_device if fits else per_device
     placed = (
         P(("hh", "per"), None),
         P(("hh", "per")),
@@ -168,7 +574,7 @@
         P("grp"),
     )
     return jax.shard_map(
-        per_device,
+        body,
         mesh=mesh,
         in_specs=placed,
         out_specs=(P(("grp", "per"), "hh", "st"), P("grp")),

time: 301 us -> 66.7 us (0.22)
  waiting for transfers between devices: 71.5 us -> 0 us
  matrix products: 63.4 us -> 0 us
  Pallas kernels: 0 us -> 55.4 us
  other arithmetic: 53.2 us -> 1.3 us
  local copies, waits for them, and re-layouts: 36.2 us -> 6.55 us
  blocking collectives: 24 us -> 0 us
  starting transfers between devices: 20 us -> 0 us
  between operations: 19 us -> 3.22 us
  loops' own time: 11.4 us -> 0 us
    dot_general x46 -> x0, matrix products: 63.4 us -> none  [the longest x16 25.6 us: forward(): jnp.dot(prev_alpha, matrix, precision=top_precision, preferred_element_ty...]
    pallas_call x0 -> x1, Pallas kernels: none -> 55.4 us  [fused_device(): pl.pallas_call(functools.partial(fused_kernel, cfg), out_shape=(jax.Shape...]
    reduce_scatter x2 -> x0, waiting for transfers between devices: 54.8 us -> none  [the longest x1 41.3 us: per_device(): lax.psum_scatter(partial_counts, 'hh', scatter_dimension=1, tiled=True)]
    psum x2 -> x0, blocking collectives: 24 us -> none  [the longest x1 21 us: per_device(): loglik_all, years_all = lax.psum((loglik_core, years_core), ('hh', 'per'))]
    select_n x35 -> x0, other arithmetic: 21.2 us -> none  [the longest x32 20.9 us: forward(): scale_now = jnp.where(seen_now, jnp.sum(joint_mass, axis=1), 1.0)]
    all_to_all x4 -> x0, starting transfers between devices: 19.9 us -> none  [the longest x1 7.28 us: per_device(): lax.all_to_all(count_out, ('hh', 'per'), split_axis=1, concat_axis=1, til...]
    dynamic_slice x31 -> x0, local copies, waits for them, and re-layouts: 18.2 us -> none  [the longest x16 9.38 us: per_device(): lax.scan(forward, start_alpha, (trans_probs, columns, period_ids))]
    all_to_all x4 -> x0, waiting for transfers between devices: 16 us -> none  [the longest x1 6.24 us: per_device(): lax.all_to_all(starts.reshape(source_rows, group_size), ('hh', 'per'), sp...]
  transfers between devices with their start and end apart: 7 -> 0, of which waited for: 5 -> 0; matrix products, arithmetic and copies ran while one was open for 5% -> 0% of each run, Pallas kernels for 0% -> 0%
where the time goes in v1:
time: 66.7 us; the launch traced here: 66.4 us
  Pallas kernels  55.4 us (83%)
  local copies, waits for them, and re-layouts  6.55 us (10%)
  between operations  3.22 us (5%)
  other arithmetic  1.3 us (2%)
    pallas_call x1, Pallas kernels, fused_device(): pl.pallas_call(functools.partial(fused_kernel, cfg), out_shape=(jax.Shape...  55.4 us
    unnamed x16, local copies, waits for them, and re-layouts  4.5 us
    concatenate x6, local copies, waits for them, and re-layouts, fused_device(): jnp.concatenate([earnings, starts.astype(F32)[:, None], lengths.astype(F3...  1.93 us

profile of v1, /device:TPU:0, one launch (start us, length us, event | category | flops | bytes accessed | tf_op | source)
XLA Modules:
  0.0 66.4 jit_solution(5262687635705618379)
XLA Ops:
  1.3 0.0 copy-start.1
  1.3 0.7 %copy-done.1 = s32[384]{0:T(512)S(1)} copy-done((s32[384]{0:T(512)S(1)}, s32[384]{0:T(512)}, u32[]{:S(2)}) %copy-start.1) | copy-done | bytes 1560
  2.0 0.6 select_reduce_fusion
  2.6 0.1 concatenate.15
  2.7 0.4 copy.13
  3.7 0.0 copy-start
  3.8 0.7 %copy-done = f32[384,16]{0,1:T(8,128)S(1)} copy-done((f32[384,16]{0,1:T(8,128)S(1)}, f32[384,16]{0,1:T(8,128)}, u32[]{:S(2)}) %copy-start) | copy-done | bytes 24600
  4.5 0.1 copy.10
  4.6 0.0 copy-start.2
  4.7 0.6 copy-done.2
  5.3 0.1 concatenate.14
  5.4 0.4 copy.12
  5.8 0.0 copy-start.4
  5.8 0.0 copy-start.5
  5.8 1.0 %concatenate.16 = f32[48,8,128]{2,0,1:T(8,128)} concatenate(f32[48,8,16]{2,0,1:T(8,128)S(1)} %copy.11, f32[48,8,1]{2,0,1:T(8,128)S(1)} %copy.12, f32[48,8,1]{2,0,1:T(8,128)S(1)} %copy.13, f32[48,8,1]{2,0,1:T(8,128)S(1)} %broadcast_in_dim.27, f32[48,8,1]{2,0,1:T(8,128)S(1)} %broadcast_in_dim.29, f32[48,8,108]{2,0,1:T(8,128)S(1)} %broadcast_in_dim.30), dimensions={2} | concatenate | bytes 393216 | tf_op jit(solution)/shard_map/concatenate | solution.py:519
  6.8 0.1 pad.3.clone
  6.9 0.0 copy-start.3
  6.9 0.0 copy-done.4
  6.9 0.0 copy-done.5
  6.9 0.7 %copy-done.3 = f32[256]{0:T(256)S(1)} copy-done((f32[256]{0:T(256)S(1)}, f32[256]{0:T(256)}, u32[]{:S(2)}) %copy-start.3) | copy-done | bytes 1048
  7.5 0.7 %maximum_maximum_fusion.par = f32[8,256]{1,0:T(8,128)} fusion(f32[1,256]{1,0:T(1,128)S(1)} %bitcast.11, f32[1,256]{1,0:T(1,128)S(1)} %bitcast.12, f32[1,256]{1,0:T(1,128)S(1)} %bitcast.13, f32[8]{0:T(128)S(1)} %pad.3.clone), kind=kLoop, calls=%fused_computation | loop fusion | flops 6144 | bytes 11296 | tf_op jit(solution)/shard_map/concatenate | solution.py:524
  8.2 55.4 %chain.1 = (f32[8,64,128]{2,1,0:T(8,128)}, f32[1,128]{1,0:T(1,128)}) custom-call(f32[8,48,128]{2,1,0:T(8,128)} %bitcast.10, bf16[4,256,256]{2,1,0:T(8,128)(2,1)} %logits.1, f32[8,256]{1,0:T(8,128)} %maximum_maximum_fusion.par), custom_call_target="tpu_custom_call" | custom-call | tf_op jit(solution)/shard_map/chain/pallas_call | solution.py:530
  63.6 0.0 copy-start.6
  63.6 1.7 %copy.17 = f32[8,64,128]{2,1,0:T(8,128)} copy(f32[8,64,128]{2,1,0:T(8,128)} %get-tuple-element.10) | data formatting | bytes 524288
  65.3 0.0 copy-done.6
  (6 shorter events, 0.1 us)
Async XLA Ops:
  1.3 0.7 %copy-start.1 = (s32[384]{0:T(512)S(1)}, s32[384]{0:T(512)}, u32[]{:S(2)}) copy-start(s32[384]{0:T(512)} %param.10) | copy-start | bytes 4612
  3.7 0.7 %copy-start = (f32[384,16]{0,1:T(8,128)S(1)}, f32[384,16]{0,1:T(8,128)}, u32[]{:S(2)}) copy-start(f32[384,16]{0,1:T(8,128)} %param.8) | copy-start | bytes 73732
  4.6 0.7 %copy-start.2 = (s32[384]{0:T(512)S(1)}, s32[384]{0:T(512)}, u32[]{:S(2)}) copy-start(s32[384]{0:T(512)} %param.9) | copy-start | bytes 4612
  5.8 1.1 %copy-start.4 = (f32[256]{0:T(256)S(1)}, f32[256]{0:T(256)}, u32[]{:S(2)}) copy-start(f32[256]{0:T(256)} %param.14) | copy-start | bytes 3076
  5.8 1.1 %copy-start.5 = (f32[256]{0:T(256)S(1)}, f32[256]{0:T(256)}, u32[]{:S(2)}) copy-start(f32[256]{0:T(256)} %param.13) | copy-start | bytes 3076
  6.9 0.7 %copy-start.3 = (f32[256]{0:T(256)S(1)}, f32[256]{0:T(256)}, u32[]{:S(2)}) copy-start(f32[256]{0:T(256)} %param.15) | copy-start | bytes 3076
  63.6 1.7 %copy-start.6 = (f32[1,128]{1,0:T(1,128)S(1)}, f32[1,128]{1,0:T(1,128)}, u32[]{:S(2)}) copy-start(f32[1,128]{1,0:T(1,128)} %get-tuple-element.5) | copy-start | bytes 1540

commit v2 on v1

--- a/solution.py
+++ b/solution.py
@@ -176,12 +176,24 @@
     return dd(ah, hi) + (dd(al, hi) + dd(ah, lo))
 
 
-def fused_kernel(cfg, pack, logits, par, out, llout,
-                 lg, got, amem, bmem, xsend, xrecv, aown, apart, uown, upart,
-                 cbuf, zrecv, llbox, rts, rtr,
+def three_way(v):
+    hi = v.astype(BF)
+    rest = v - hi.astype(F32)
+    mid = rest.astype(BF)
+    return hi, mid, (rest - mid.astype(F32)).astype(BF)
+
+
+def sum3(pieces, right, dims):
+    dd = lambda p: lax.dot_general(p, right, (dims, ((), ())), preferred_element_type=F32)
+    return (dd(pieces[0]) + dd(pieces[1])) + dd(pieces[2])
+
+
+def fused_kernel(cfg, earn, begin, length, count, logits, init_ref, mean_ref, sd_ref, out, llout,
+                 pack, lg, got, amem, bmem, xsend, xrecv, aown, apart, uown, upart,
+                 cbuf, zrecv, zmid, zfar, llbox, rts, rtr,
                  gsend, grecv, lrecv, lsend_p, lsend_x, lsend_r,
                  xs_sem, xr_sem, as_sem, ar_sem, us_sem, ur_sem,
-                 zs_sem, zr_sem, lls_sem, llr_sem, rs_sem, rr_sem):
+                 zs_sem, zr_sem, zfs_sem, zfr_sem, lls_sem, llr_sem, rs_sem, rr_sem):
     nz, nt, half_t, own_t, rows, num_states = cfg
     x = lax.axis_index("per")
     z = lax.axis_index("hh")
@@ -189,7 +201,8 @@
     half = num_states // 2
     nsrc = nz * 2
     zr = num_states // nz
-    slab = pack.shape[1]
+    slots = earn.shape[1]
+    slab = slots // nsrc
 
     def rcopy(src, dst, ss, rs, dev):
         return pltpu.make_async_remote_copy(
@@ -208,10 +221,29 @@
                     others.append({"hh": lax.rem(z + dz, nz), "per": lax.rem(x + dx, 2), "st": lax.rem(s + ds, 2)})
     for dev in others:
         pl.semaphore_signal(barrier, inc=1, device_id=dev, device_id_type=MESH)
+
+    cnt = count[0].astype(F32)
+    spot = lax.broadcasted_iota(jnp.int32, (1, slots), 1).astype(F32)
+    lens = length[...].astype(F32)
+    own_years = jnp.sum(jnp.where(spot < cnt * float(rows), lens, 0.0), axis=1, keepdims=True)
+    table = jnp.concatenate(
+        [earn[...], begin[...].astype(F32), lens, jnp.full((1, slots), 1.0, F32) * cnt,
+         jnp.broadcast_to(own_years, (1, slots)), jnp.zeros((4, slots), F32)], axis=0)
+    pieces = three_way(table)
+    q_id = lax.broadcasted_iota(jnp.int32, (slots, 128), 0)
+    r_id = lax.broadcasted_iota(jnp.int32, (slots, 128), 1)
+    for tz in range(nz):
+        pick = jnp.where((q_id == r_id * nsrc + (tz * 2 + s)) & (r_id < slab), 1.0, 0.0).astype(BF)
+        pack[tz] = sum3(pieces, pick, ((1,), (0,)))
     pl.semaphore_wait(barrier, len(others))
 
     partner = {"hh": z, "per": x, "st": 1 - s}
     across = {"hh": z, "per": 1 - x, "st": s}
+    near_z = z + 1 - 2 * lax.rem(z, 2)
+    near_par = lax.rem(near_z, 2)
+    far_z = lax.rem(z + 2, 4)
+    near = {"hh": near_z, "per": x, "st": s}
+    far = {"hh": far_z, "per": x, "st": s}
 
     me_src = z * 2 + x
     hist = []
@@ -220,9 +252,9 @@
         for dx in range(2):
             tz, tx = lax.rem(z + dz, nz), lax.rem(x + dx, 2)
             if dz == 0 and dx == 0:
-                c = pltpu.make_async_copy(pack.at[tz * 2 + s], got.at[me_src], grecv.at[0])
+                c = pltpu.make_async_copy(pack.at[tz], got.at[me_src], grecv.at[0])
             else:
-                c = rcopy(pack.at[tz * 2 + s], got.at[me_src], gsend.at[n], grecv.at[n],
+                c = rcopy(pack.at[tz], got.at[me_src], gsend.at[n], grecv.at[n],
                           {"hh": tz, "per": tx, "st": s})
             c.start()
             hist.append(c)
@@ -232,12 +264,12 @@
     sends = []
     for i in range(own_t):
         off = jnp.where(x == 0, own_t - 1 - i, i)
-        near = own_t - 1 - off
-        p = mine + near
-        c = rcopy(logits.at[near], lg.at[p], lsend_p.at[i], lrecv.at[p], partner)
+        back_off = own_t - 1 - off
+        p = mine + back_off
+        c = rcopy(logits.at[back_off], lg.at[p], lsend_p.at[i], lrecv.at[p], partner)
         c.start()
         sends.append(c)
-        c = pltpu.make_async_copy(logits.at[near], lg.at[p], lrecv.at[p])
+        c = pltpu.make_async_copy(logits.at[back_off], lg.at[p], lrecv.at[p])
         c.start()
     for i in range(own_t):
         off = jnp.where(x == 0, own_t - 1 - i, i)
@@ -246,9 +278,9 @@
         c.start()
         sends.append(c)
 
-    init = par[0:1, :]
-    mean = par[1:2, :]
-    log_sd = par[2:3, :]
+    init = init_ref[...]
+    mean = mean_ref[...]
+    log_sd = sd_ref[...]
     raised_first = jnp.exp(init)
     first = raised_first / jnp.sum(raised_first, axis=1, keepdims=True)
     inv_sd = jnp.exp(-log_sd)
@@ -260,18 +292,19 @@
             hist[n].wait_recv()
     base = jnp.zeros((1, 1), F32)
     years = jnp.zeros((1, 1), F32)
-    picked = jnp.zeros((rows, 128), F32)
-    lane = lax.broadcasted_iota(jnp.int32, (slab, rows), 1).astype(F32)
-    sub = lax.broadcasted_iota(jnp.int32, (slab, rows), 0).astype(F32)
+    seat = lax.broadcasted_iota(jnp.int32, (rows, 128), 0).astype(F32)
+    lane = lax.broadcasted_iota(jnp.int32, (rows, 128), 1).astype(F32)
+    hots = []
     for src in range(nsrc):
-        g = got[src]
-        live = g[0:1, nt + 2:nt + 3] * float(rows // nsrc)
-        years = years + g[0:1, nt + 3:nt + 4]
-        onehot = jnp.where((sub + base == lane) & (sub < live), 1.0, 0.0)
-        picked = picked + lax.dot_general(
-            onehot, g, (((0,), (0,)), ((), ())),
-            precision=lax.Precision.HIGHEST, preferred_element_type=F32)
+        live = got[src, nt + 2:nt + 3, 0:1] * float(rows // nsrc)
+        years = years + got[src, nt + 3:nt + 4, 0:1]
+        hots.append(jnp.where((lane + base == seat) & (lane < live), 1.0, 0.0).astype(BF))
         base = base + live
+    hot = jnp.concatenate(hots, axis=1)
+    wide = jnp.concatenate([got[src] for src in range(nsrc)], axis=1)
+    dd = lambda g: lax.dot_general(hot, g, (((1,), (1,)), ((), ())), preferred_element_type=F32)
+    g0, g1, g2 = three_way(wide)
+    picked = (dd(g0) + dd(g1)) + dd(g2)
     start = picked[:, nt:nt + 1]
     stop = start + picked[:, nt + 1:nt + 2]
 
@@ -335,18 +368,38 @@
             a_all = jnp.concatenate([a_ref[k, b], apart[k, b]], axis=0)
             cbuf[k, b * half:(b + 1) * half, :] = lax.dot_general(
                 a_all, u_all, (((0,), (0,)), ((), ())), preferred_element_type=F32)
-        for dz in range(1, nz):
-            tz = lax.rem(z + dz, nz)
-            rcopy(cbuf.at[k, pl.ds(pl.multiple_of(tz * zr, 8), zr)], zrecv.at[dz - 1, k],
-                  zs_sem.at[dz - 1, k], zr_sem.at[dz - 1, k],
-                  {"hh": tz, "per": x, "st": s}).start()
-
-    relay_at = {2: 0, 4: 1, 6: 2, 8: 3}
+        for j in range(2):
+            rcopy(cbuf.at[k, pl.ds(pl.multiple_of((near_par + 2 * j) * zr, 8), zr)], zrecv.at[j, k],
+                  zs_sem.at[j, k], zr_sem.at[j, k], near).start()
+
+    def stage_three(k):
+        for j in range(2):
+            arrived(zrecv.at[j, k], zr_sem.at[j, k])
+        here, there = z // 2, 1 - z // 2
+        zmid[k] = zrecv[here, k] + cbuf[k, pl.ds(pl.multiple_of(z * zr, 8), zr), :]
+        cbuf[k, pl.ds(pl.multiple_of(far_z * zr, 8), zr), :] = (
+            zrecv[there, k] + cbuf[k, pl.ds(pl.multiple_of(far_z * zr, 8), zr), :])
+        rcopy(cbuf.at[k, pl.ds(pl.multiple_of(far_z * zr, 8), zr)], zfar.at[k],
+              zfs_sem.at[k], zfr_sem.at[k], far).start()
+
+    def advance(xs, todo, ready, summed):
+        if len(summed) > 1 or (summed and not ready):
+            stage_three(summed.pop(0))
+        if ready:
+            k = ready.pop(0)
+            stage_two(k, xs)
+            summed.append(k)
+        if todo:
+            k = todo.pop(0)
+            stage_one(k, xs)
+            ready.append(k)
+
+    relay_at = {1: 0, 3: 1, 5: 2, 7: 3}
 
     @pl.when(x == 0)
     def _forward():
         todo = list(range(half_t - 1, 0, -1))
-        ready = []
+        ready, summed = [], []
         total = jnp.zeros((rows, 1), F32)
         joint = scale_inv = None
         for t in range(nt):
@@ -355,14 +408,19 @@
             e = emit(t)
             if t == 0:
                 need(0, 0)
+                need(1, 0)
                 joint = first * e
+                hi, lo = probs(1)
             else:
-                need(t, 0)
-                hi, lo = probs(t)
+                if t + 1 < nt:
+                    need(t + 1, 0)
+                    nxt = probs(t + 1)
                 moved = dot3(joint, hi, lo, ((1,), (0,))) * scale_inv
                 if t < half_t:
                     bmem[t] = moved
                 joint = jnp.where(float(t) <= start, first, moved) * e
+                if t + 1 < nt:
+                    hi, lo = nxt
             scale = jnp.sum(joint, axis=1, keepdims=True)
             seen = (float(t) >= start) & (float(t) < stop)
             total = total + jnp.where(seen, jnp.log(scale), 0.0)
@@ -372,37 +430,31 @@
             elif t < nt - 1:
                 send_across(t - (half_t - 1), joint * scale_inv)
             if t >= half_t + 1:
-                if ready:
-                    stage_two(ready.pop(0), 0)
-                if todo:
-                    k = todo.pop(0)
-                    stage_one(k, 0)
-                    ready.append(k)
+                advance(0, todo, ready, summed)
         llsum = jnp.sum(total, axis=0, keepdims=True)
         llbox[z * 2 + s] = jnp.broadcast_to(llsum, (8, 128))
         for j, dev in enumerate(others):
             rcopy(llbox.at[z * 2 + s], llbox.at[z * 2 + s], lls_sem.at[j], llr_sem.at[z * 2 + s], dev).start()
-        while todo or ready:
-            if ready:
-                stage_two(ready.pop(0), 0)
-            if todo:
-                k = todo.pop(0)
-                stage_one(k, 0)
-                ready.append(k)
+        while todo or ready or summed:
+            advance(0, todo, ready, summed)
         for j, dev in enumerate(others):
             rcopy(llbox.at[z * 2 + s], llbox.at[z * 2 + s], lls_sem.at[j], llr_sem.at[z * 2 + s], dev).wait_send()
 
     @pl.when(x == 1)
     def _backward():
         todo = list(range(half_t))
-        ready = []
+        ready, summed = [], []
         back = jnp.ones((rows, num_states), F32)
         for step in range(nt - 1):
             t = nt - 1 - step
             if step in relay_at:
                 relay(relay_at[step], 1)
-            need(t, 1)
-            hi, lo = probs(t)
+            if step == 0:
+                need(t, 1)
+                hi, lo = probs(t)
+            if t > 2:
+                need(t - 1, 1)
+                nxt = probs(t - 1)
             v = emit(t) * back
             norm_inv = 1.0 / jnp.sum(v, axis=1, keepdims=True)
             mv = moving(t)
@@ -415,21 +467,14 @@
                 back = jnp.where(mv, dot3(v, hi, lo, ((1,), (1,))) * norm_inv, 1.0)
                 if t >= half_t:
                     bmem[t - half_t] = back
+                if t > 2:
+                    hi, lo = nxt
             if step >= half_t + 1:
-                if ready:
-                    stage_two(ready.pop(0), 1)
-                if todo:
-                    k = todo.pop(0)
-                    stage_one(k, 1)
-                    ready.append(k)
+                advance(1, todo, ready, summed)
+        need(1, 1)
         need(0, 1)
-        while todo or ready:
-            if ready:
-                stage_two(ready.pop(0), 1)
-            if todo:
-                k = todo.pop(0)
-                stage_one(k, 1)
-                ready.append(k)
+        while todo or ready or summed:
+            advance(1, todo, ready, summed)
 
     zrow = pl.ds(pl.multiple_of(z * zr, 8), zr)
     col = pl.ds(pl.multiple_of(s * half, 128), half)
@@ -441,11 +486,8 @@
 
         @pl.when(q > 0)
         def _():
-            for d in range(nz - 1):
-                arrived(zrecv.at[d, k], zr_sem.at[d, k])
-            c = cbuf[k, zrow, :]
-            for d in range(nz - 1):
-                c = c + zrecv[d, k]
+            arrived(zfar.at[k], zfr_sem.at[k])
+            c = zmid[k] + zfar[k]
             r = jnp.exp(lg[q, zrow, :].astype(F32))
             mine_r = jnp.exp(lg[q, zrow, col].astype(F32))
             bmem[k, 0:zr, 0:half] = mine_r / jnp.sum(r, axis=1, keepdims=True)
@@ -487,8 +529,9 @@
         def drain(k=k):
             rcopy(aown.at[k], apart.at[k], as_sem.at[k], ar_sem.at[k], partner).wait_send()
             rcopy(uown.at[k, 0], upart.at[k], us_sem.at[k], ur_sem.at[k], partner).wait_send()
-            for d in range(nz - 1):
-                rcopy(cbuf.at[k, pl.ds(0, zr)], zrecv.at[d, k], zs_sem.at[d, k], zr_sem.at[d, k], partner).wait_send()
+            for d in range(2):
+                rcopy(cbuf.at[k, pl.ds(0, zr)], zrecv.at[d, k], zs_sem.at[d, k], zr_sem.at[d, k], near).wait_send()
+            rcopy(cbuf.at[k, pl.ds(0, zr)], zfar.at[k], zfs_sem.at[k], zfr_sem.at[k], far).wait_send()
         if k == 0:
             pl.when(x == 1)(drain)
             @pl.when(x == 0)
@@ -513,16 +556,6 @@
     half = num_states // 2
     zr = num_states // nz
     rows = HB
-    count = block_count.astype(F32)[0]
-    live = jnp.arange(slot_rows, dtype=jnp.int32) < block_count[0] * HB
-    years = jnp.sum(jnp.where(live, lengths, 0)).astype(F32)
-    pack = jnp.concatenate(
-        [earnings, starts.astype(F32)[:, None], lengths.astype(F32)[:, None],
-         jnp.broadcast_to(count, (slot_rows, 1)), jnp.broadcast_to(years, (slot_rows, 1)),
-         jnp.zeros((slot_rows, 128 - nt - 4), F32)], axis=1)
-    pack = pack.reshape(slab, nsrc, 128).transpose(1, 0, 2)
-    par = jnp.concatenate(
-        [init_logits[None], state_mean[None], log_sd[None], jnp.zeros((5, num_states), F32)], axis=0)
     cfg = (nz, nt, half_t, own_t, rows, num_states)
     V = pltpu.VMEM
     D = pltpu.SemaphoreType.DMA
@@ -531,11 +564,12 @@
         functools.partial(fused_kernel, cfg),
         out_shape=(jax.ShapeDtypeStruct((half_t, zr, half), F32),
                    jax.ShapeDtypeStruct((1, 128), F32)),
-        in_specs=[vm] * 3,
+        in_specs=[vm, vm, vm, pl.BlockSpec(memory_space=pltpu.SMEM), pl.BlockSpec(memory_space=pl.ANY), vm, vm, vm],
         out_specs=(vm, vm),
         scratch_shapes=[
+            V((nz, nt + 8, 128), F32),
             V((nt, num_states, num_states), BF),
-            V((nsrc, slab, 128), F32),
+            V((nsrc, nt + 8, 128), F32),
             V((half_t, rows, num_states), F32),
             V((half_t, rows, num_states), F32),
             V((half_t, 2, rows, half), BF),
@@ -545,23 +579,26 @@
             V((half_t, 2, rows, half), BF),
             V((half_t, rows, half), BF),
             V((half_t, num_states, half), F32),
-            V((nz - 1, half_t, zr, half), F32),
+            V((2, half_t, zr, half), F32),
+            V((half_t, zr, half), F32),
+            V((half_t, zr, half), F32),
             V((nsrc, 8, 128), F32),
             V((zr, 128), F32),
             V((zr, 128), F32),
             D((nsrc,)), D((nsrc,)), D((nt,)), D((own_t,)), D((own_t,)), D((own_t,)),
             D((half_t,)), D((half_t,)), D((half_t,)), D((half_t,)), D((half_t,)), D((half_t,)),
-            D((nz - 1, half_t)), D((nz - 1, half_t)), D((4 * nz,)), D((nsrc,)), D((1,)), D((1,)),
+            D((2, half_t)), D((2, half_t)), D((half_t,)), D((half_t,)), D((4 * nz,)), D((nsrc,)), D((1,)), D((1,)),
         ],
         compiler_params=pltpu.CompilerParams(
             collective_id=0, has_side_effects=True, vmem_limit_bytes=56 * 1024 * 1024),
         name="chain",
-    )(pack, trans_logits, par)
+    )(earnings.T, starts[None], lengths[None], block_count, trans_logits,
+      init_logits[None], state_mean[None], log_sd[None])
     return grad, ll[0, 0:1]
 
 
 def solution(mesh):
-    fits = mesh.shape["per"] == 2 and mesh.shape["st"] == 2 and HB % (mesh.shape["hh"] * 2) == 0
+    fits = mesh.shape["per"] == 2 and mesh.shape["st"] == 2 and mesh.shape["hh"] == 4
     body = fused_device if fits else per_device
     placed = (
         P(("hh", "per"), None),

time: 66.7 us -> 57.5 us (0.86)
  Pallas kernels: 55.4 us -> 51.1 us
  local copies, waits for them, and re-layouts: 6.55 us -> 3.62 us
  other arithmetic: 1.3 us -> 0 us
  between operations: 3.22 us -> 2.47 us
    pallas_call x1, Pallas kernels: 55.4 us -> 51.1 us  [fused_device(): pl.pallas_call(functools.partial(fused_kernel, cfg), out_shape=(jax.Shape...]
    unnamed x16 -> x7, local copies, waits for them, and re-layouts: 4.5 us -> 2.47 us
    concatenate x7 -> x0, local copies, waits for them, and re-layouts: 2 us -> none  [the longest x6 1.93 us: fused_device(): jnp.concatenate([earnings, starts.astype(F32)[:, None], lengths.astype(F3...]
    broadcast_in_dim x4 -> x2, local copies, waits for them, and re-layouts: 0.04 us -> 1.15 us  [the longest x1 0.59 us: fused_device(): lengths[None]]
where the time goes in v2:
time: 57.5 us; the launch traced here: 57.2 us
  Pallas kernels  51.1 us (89%)
  local copies, waits for them, and re-layouts  3.62 us (6%)
  between operations  2.47 us (4%)
    pallas_call x1, Pallas kernels, fused_device(): pl.pallas_call(functools.partial(fused_kernel, cfg), out_shape=(jax.Shape...  51.1 us
    unnamed x7, local copies, waits for them, and re-layouts  2.47 us

profile of v2, /device:TPU:0, one launch (start us, length us, event | category | flops | bytes accessed | tf_op | source)
XLA Modules:
  0.0 57.2 jit_solution(862670724832476277)
XLA Ops:
  1.3 0.0 copy-start
  1.3 0.7 %copy-done = s32[384]{0:T(512)S(1)} copy-done((s32[384]{0:T(512)S(1)}, s32[384]{0:T(512)}, u32[]{:S(2)}) %copy-start) | copy-done | bytes 1560
  2.0 0.0 copy-start.1
  2.0 0.6 broadcast_in_dim.15.begin
  2.5 0.1 copy-done.1
  2.6 0.6 %broadcast_in_dim.16.length = s32[1,384]{1,0:T(1,128)} reshape(s32[384]{0:T(512)S(1)} %copy-done.1) | data formatting | bytes 3072 | tf_op jit(solution)/shard_map/broadcast_in_dim | solution.py:595
  3.2 51.1 %chain.1 = (f32[8,64,128]{2,1,0:T(8,128)}, f32[1,128]{1,0:T(1,128)}) custom-call(f32[16,384]{1,0:T(8,128)} %bitcast.6, s32[1,384]{1,0:T(1,128)} %broadcast_in_dim.15.begin, s32[1,384]{1,0:T(1,128)} %broadcast_in_dim.16.length, s32[1]{0:T(128)S(6)} %copy.12.count, bf16[4,256,256]{2,1,0:T(8,128)(2,1)} %logits.1, f32[1,256]{1,0:T(1,128)} %bitcast.7, ...), custom_call_target="tpu_custom_call" | custom-call | tf_op jit(solution)/shard_map/chain/pallas_call | solution.py:563
  54.3 0.0 copy-start.2
  54.4 1.7 %copy.13 = f32[8,64,128]{2,1,0:T(8,128)} copy(f32[8,64,128]{2,1,0:T(8,128)} %get-tuple-element.8) | data formatting | bytes 524288
  56.0 0.0 copy-done.2
Async XLA Ops:
  1.3 0.7 %copy-start = (s32[384]{0:T(512)S(1)}, s32[384]{0:T(512)}, u32[]{:S(2)}) copy-start(s32[384]{0:T(512)} %param.9) | copy-start | bytes 4612
  2.0 0.7 %copy-start.1 = (s32[384]{0:T(512)S(1)}, s32[384]{0:T(512)}, u32[]{:S(2)}) copy-start(s32[384]{0:T(512)} %param.10) | copy-start | bytes 4612
  54.3 1.7 %copy-start.2 = (f32[1,128]{1,0:T(1,128)S(1)}, f32[1,128]{1,0:T(1,128)}, u32[]{:S(2)}) copy-start(f32[1,128]{1,0:T(1,128)} %get-tuple-element.5) | copy-start | bytes 1540

commit v3 on v0

--- a/solution.py
+++ b/solution.py
@@ -1,7 +1,11 @@
+import functools
+
 import jax
 import jax.numpy as jnp
 from jax import lax
 from jax.sharding import PartitionSpec as P
+from jax.experimental import pallas as pl
+from jax.experimental.pallas import tpu as pltpu
 
 HB = 128
 
@@ -156,7 +160,347 @@
     return (trans_grad, mean_loglik)
 
 
+F32 = jnp.float32
+BF = jnp.bfloat16
+MESH = pl.DeviceIdType.MESH
+
+
+def split_hi_lo(v):
+    hi = v.astype(BF)
+    return hi, (v - hi.astype(F32)).astype(BF)
+
+
+def dot3(a, hi, lo, dims):
+    ah, al = split_hi_lo(a)
+    dd = lambda p, q: lax.dot_general(p, q, (dims, ((), ())), preferred_element_type=F32)
+    return dd(ah, hi) + (dd(al, hi) + dd(ah, lo))
+
+
+def three_way(v):
+    hi = v.astype(BF)
+    rest = v - hi.astype(F32)
+    mid = rest.astype(BF)
+    return hi, mid, (rest - mid.astype(F32)).astype(BF)
+
+
+def sum3(pieces, right, dims):
+    dd = lambda p: lax.dot_general(p, right, (dims, ((), ())), preferred_element_type=F32)
+    return (dd(pieces[0]) + dd(pieces[1])) + dd(pieces[2])
+
+
+def fused_kernel(cfg, earn, begin, length, count, logits, init_ref, mean_ref, sd_ref, out, llout,
+                 pack, got, people, lg, phi, plo, amem, bmem, xsend, xrecv, cacc, crecv,
+                 llbox, rts, rtr,
+                 hs_sem, hr_sem, lr_sem, ls_sem, xs_sem, xr_sem, c_sem, r_sem, lls_sem, llr_sem):
+    nz, nt, half_t, own_t, rows, num_states, blocks = cfg
+    x = lax.axis_index("per")
+    z = lax.axis_index("hh")
+    s = lax.axis_index("st")
+    half = num_states // 2
+    nsrc = nz * 2
+    zr = num_states // nz
+    per_half = half // zr
+    slots = earn.shape[1]
+    slab = slots // 2
+    wide_slab = pack.shape[1]
+
+    def rcopy(src, dst, ss, rs, dev):
+        return pltpu.make_async_remote_copy(
+            src_ref=src, dst_ref=dst, send_sem=ss, recv_sem=rs,
+            device_id=dev, device_id_type=MESH)
+
+    partner = {"hh": z, "per": x, "st": 1 - s}
+    across = {"hh": z, "per": 1 - x, "st": s}
+    corner = {"hh": z, "per": 1 - x, "st": 1 - s}
+    peers = []
+    for dz in range(nz):
+        for dx in range(2):
+            if dz or dx:
+                peers.append({"hh": lax.rem(z + dz, nz), "per": lax.rem(x + dx, 2), "st": s})
+    barrier = pltpu.get_barrier_semaphore()
+    for dev in peers + [partner, corner]:
+        pl.semaphore_signal(barrier, inc=1, device_id=dev, device_id_type=MESH)
+
+    local = []
+    for i in range(own_t):
+        c = pltpu.make_async_copy(logits.at[i], lg.at[own_t * s + i], lr_sem.at[i])
+        c.start()
+        local.append(c)
+
+    cnt = count[0].astype(F32)
+    spot = lax.broadcasted_iota(jnp.int32, (1, slots), 1).astype(F32)
+    lens = length[...].astype(F32)
+    own_years = jnp.sum(jnp.where(spot < cnt * float(rows), lens, 0.0), axis=1, keepdims=True)
+    table = jnp.concatenate(
+        [earn[...], begin[...].astype(F32), lens, jnp.full((1, slots), 1.0, F32) * cnt,
+         jnp.broadcast_to(own_years, (1, slots)), jnp.zeros((4, slots), F32)], axis=0)
+    q_id = lax.broadcasted_iota(jnp.int32, (slots, wide_slab), 0)
+    r_id = lax.broadcasted_iota(jnp.int32, (slots, wide_slab), 1)
+    pick = jnp.where((q_id == r_id * 2 + s) & (r_id < slab), 1.0, 0.0).astype(BF)
+    pack[...] = sum3(three_way(table), pick, ((1,), (0,)))
+    pl.semaphore_wait(barrier, len(peers) + 2)
+
+    me_src = z * 2 + x
+    hist = [pltpu.make_async_copy(pack, got.at[me_src], hr_sem.at[0])]
+    hist[0].start()
+    for n, dev in enumerate(peers):
+        c = rcopy(pack, got.at[me_src], hs_sem.at[n], hr_sem.at[n + 1], dev)
+        c.start()
+        hist.append(c)
+    near = []
+    for i in range(own_t):
+        c = rcopy(logits.at[i], lg.at[own_t * s + i], ls_sem.at[i], lr_sem.at[own_t + i], partner)
+        c.start()
+        near.append(c)
+
+    mean = mean_ref[...]
+    log_sd = sd_ref[...]
+    raised_first = jnp.exp(init_ref[...])
+    first = raised_first / jnp.sum(raised_first, axis=1, keepdims=True)
+    inv_sd = jnp.exp(-log_sd)
+
+    def make_probs(l):
+        r = jnp.exp(lg[l].astype(F32))
+        hi, lo = split_hi_lo(r / jnp.sum(r, axis=1, keepdims=True))
+        phi[l] = hi
+        plo[l] = lo
+
+    for i in range(own_t):
+        local[i].wait()
+        make_probs(own_t * s + i)
+    cacc[...] = jnp.zeros(cacc.shape, F32)
+    for i in range(own_t):
+        near[i].wait_recv()
+        make_probs(own_t * (1 - s) + i)
+
+    hist[0].wait()
+    for n in range(len(peers)):
+        hist[n + 1].wait_recv()
+    base = jnp.zeros((1, 1), F32)
+    years = jnp.zeros((1, 1), F32)
+    bases, lives = [], []
+    for src in range(nsrc):
+        live = got[src, nt + 2:nt + 3, 0:1] * float(rows // 2)
+        years = years + got[src, nt + 3:nt + 4, 0:1]
+        bases.append(base)
+        lives.append(live)
+        base = base + live
+    g0, g1, g2 = three_way(jnp.concatenate([got[src] for src in range(nsrc)], axis=1))
+    seat = lax.broadcasted_iota(jnp.int32, (rows, wide_slab), 0).astype(F32)
+    lane = lax.broadcasted_iota(jnp.int32, (rows, wide_slab), 1).astype(F32)
+    for b in range(blocks):
+        hot = jnp.concatenate(
+            [jnp.where((lane + (bases[src] - float(b * rows)) == seat) & (lane < lives[src]), 1.0, 0.0).astype(BF)
+             for src in range(nsrc)], axis=1)
+        dd = lambda g: lax.dot_general(hot, g, (((1,), (1,)), ((), ())), preferred_element_type=F32)
+        people[b, :, 0:nt + 8] = (dd(g0) + dd(g1)) + dd(g2)
+
+    def emit(b, t):
+        zs = (people[b, :, t:t + 1] - mean) * inv_sd
+        return jnp.exp(-0.5 * zs * zs - log_sd)
+
+    def span(b):
+        start = people[b, :, nt:nt + 1]
+        return start, start + people[b, :, nt + 1:nt + 2]
+
+    def add_counts(k, a, u):
+        part = lax.dot_general(a.astype(BF), u.astype(BF), (((0,), (0,)), ((), ())),
+                               preferred_element_type=F32)
+        cacc[k, 0] += part[:, :half]
+        cacc[k, 1] += part[:, half:]
+
+    def send_across(b, v):
+        xsend[b] = v.astype(BF)
+        rcopy(xsend.at[b], xrecv.at[b], xs_sem.at[b], xr_sem.at[b], across).start()
+
+    def take_across(b):
+        c = rcopy(xsend.at[b], xrecv.at[b], xs_sem.at[b], xr_sem.at[b], across)
+        c.wait_recv()
+        return xrecv[b].astype(F32)
+
+    def chosen(v):
+        return jnp.where(z // per_half == 0, v[:, :half], v[:, half:])
+
+    def forward_step(b, t, prev, prev_inv, total, start, stop):
+        e = emit(b, t)
+        moved = None
+        if t == 0:
+            joint = first * e
+        else:
+            l = t % half_t
+            moved = dot3(prev, phi[l], plo[l], ((1,), (0,))) * prev_inv
+            joint = jnp.where(float(t) <= start, first, moved) * e
+        scale = jnp.sum(joint, axis=1, keepdims=True)
+        seen = (float(t) >= start) & (float(t) < stop)
+        total = total + jnp.where(seen, jnp.log(scale), 0.0)
+        return joint, 1.0 / scale, total, moved
+
+    def backward_step(b, t, back, start, stop, last):
+        v = emit(b, t) * back
+        norm_inv = 1.0 / jnp.sum(v, axis=1, keepdims=True)
+        mv = (float(t) > start) & (float(t) < stop)
+        u = jnp.where(mv, v * norm_inv, 0.0)
+        if not last:
+            l = t % half_t
+            back = jnp.where(mv, dot3(v, phi[l], plo[l], ((1,), (1,))) * norm_inv, 1.0)
+        return u, back, mv
+
+    def weight(mv, zsum):
+        return jnp.where(mv, 1.0 / jnp.where(mv, zsum, 1.0), 0.0)
+
+    def put_ll(total):
+        llbox[x * 2 + s] = jnp.broadcast_to(jnp.sum(total, axis=0, keepdims=True), (8, 128))
+
+    @pl.when(x == 0)
+    def _early():
+        def one(b, total):
+            start, stop = span(b)
+            prev = prev_inv = None
+            for t in range(half_t):
+                prev, prev_inv, total, moved = forward_step(b, t, prev, prev_inv, total, start, stop)
+                if t > 0:
+                    bmem[b, t] = moved
+                if t < half_t - 1:
+                    amem[b, t + 1, :, 0:half] = chosen(prev) * prev_inv
+            send_across(b, prev * prev_inv)
+            return total
+
+        put_ll(lax.fori_loop(0, blocks, one, jnp.zeros((rows, 1), F32)))
+
+        def two(b, carry):
+            start, stop = span(b)
+            back = take_across(b)
+            for t in range(half_t - 1, 0, -1):
+                u, back, mv = backward_step(b, t, back, start, stop, t == 1)
+                w = weight(mv, jnp.sum(bmem[b, t] * u, axis=1, keepdims=True))
+                add_counts(t, amem[b, t, :, 0:half] * w, u)
+            return carry
+
+        lax.fori_loop(0, blocks, two, 0)
+
+    @pl.when(x == 1)
+    def _late():
+        def one(b, carry):
+            start, stop = span(b)
+            back = jnp.ones((rows, num_states), F32)
+            for t in range(nt - 1, half_t - 1, -1):
+                u, back, mv = backward_step(b, t, back, start, stop, False)
+                amem[b, t - half_t] = u
+                bmem[b, t - half_t] = back
+            send_across(b, back)
+            return carry
+
+        lax.fori_loop(0, blocks, one, 0)
+
+        def two(b, total):
+            start, stop = span(b)
+            prev = take_across(b)
+            prev_inv = jnp.ones((rows, 1), F32)
+            for t in range(half_t, nt):
+                alpha = prev * prev_inv
+                mv = (float(t) > start) & (float(t) < stop)
+                w = weight(mv, jnp.sum(bmem[b, t - half_t] * alpha, axis=1, keepdims=True))
+                add_counts(t - half_t, chosen(alpha) * w, amem[b, t - half_t])
+                prev, prev_inv, total, moved = forward_step(b, t, prev, prev_inv, total, start, stop)
+            return total
+
+        put_ll(lax.fori_loop(0, blocks, two, jnp.zeros((rows, 1), F32)))
+
+    mine = x * 2 + s
+    ll_to = [(partner, x * 2 + 1 - s), (across, (1 - x) * 2 + s), (corner, (1 - x) * 2 + 1 - s)]
+    ll_copies = []
+    for j, (dev, there) in enumerate(ll_to):
+        c = rcopy(llbox.at[mine], llbox.at[mine], lls_sem.at[j], llr_sem.at[j], dev)
+        c.start()
+        ll_copies.append(c)
+    zrow = pl.ds(pl.multiple_of(lax.rem(z, per_half) * zr, 8), zr)
+    prow = pl.ds(pl.multiple_of(z * zr, 8), zr)
+    cc = rcopy(cacc.at[:, 1 - s, zrow], crecv, c_sem.at[0], c_sem.at[1], partner)
+    cc.start()
+    lane_out = lax.broadcasted_iota(jnp.int32, (zr, 128), 1)
+    sums = jnp.zeros((zr, 128), F32)
+    for k in range(half_t):
+        r = jnp.exp(lg[k, prow, :].astype(F32))
+        pr = r / jnp.sum(r, axis=1, keepdims=True)
+        row = jnp.sum(pr[:, :half] * cacc[k, 0, zrow, :] + pr[:, half:] * cacc[k, 1, zrow, :],
+                      axis=1, keepdims=True)
+        sums = sums + jnp.where(lane_out == k, row, 0.0)
+        out[k] = jnp.where(s == 0, pr[:, :half], pr[:, half:])
+    rts[...] = sums
+    rc = rcopy(rts, rtr, r_sem.at[0], r_sem.at[1], partner)
+    rc.start()
+    factor = float(num_states * num_states * nt) / years
+    cc.wait_recv()
+    rc.wait_recv()
+    rtot = rts[...] + rtr[...]
+    for k in range(half_t):
+        out[k] = factor * (out[k] * ((cacc[k, s, zrow, :] + crecv[k]) - rtot[:, k:k + 1]))
+    for c in ll_copies:
+        c.wait_recv()
+    ll = (llbox[0, 0:1, :] + llbox[1, 0:1, :]) + (llbox[2, 0:1, :] + llbox[3, 0:1, :])
+    llout[...] = ll / years
+
+    for c in hist[1:] + near + ll_copies + [cc, rc]:
+        c.wait_send()
+    for b in range(blocks):
+        rcopy(xsend.at[b], xrecv.at[b], xs_sem.at[b], xr_sem.at[b], across).wait_send()
+
+
+def fused_device(
+    earnings, starts, lengths, block_count, trans_logits, init_logits, state_mean, log_sd
+):
+    num_states = init_logits.shape[0]
+    nt = earnings.shape[1]
+    slot_rows = earnings.shape[0]
+    nz = lax.axis_size("hh")
+    nsrc = nz * 2
+    own_t = trans_logits.shape[0]
+    half_t = nt // 2
+    half = num_states // 2
+    zr = num_states // nz
+    rows = HB
+    blocks = nsrc // 2
+    wide_slab = -(-(slot_rows // 2) // 128) * 128
+    cfg = (nz, nt, half_t, own_t, rows, num_states, blocks)
+    V = pltpu.VMEM
+    D = pltpu.SemaphoreType.DMA
+    vm = pl.BlockSpec(memory_space=pltpu.VMEM)
+    grad, ll = pl.pallas_call(
+        functools.partial(fused_kernel, cfg),
+        out_shape=(jax.ShapeDtypeStruct((half_t, zr, half), F32),
+                   jax.ShapeDtypeStruct((1, 128), F32)),
+        in_specs=[vm, vm, vm, pl.BlockSpec(memory_space=pltpu.SMEM), pl.BlockSpec(memory_space=pl.ANY), vm, vm, vm],
+        out_specs=(vm, vm),
+        scratch_shapes=[
+            V((nt + 8, wide_slab), F32),
+            V((nsrc, nt + 8, wide_slab), F32),
+            V((blocks, rows, 128), F32),
+            V((half_t, num_states, num_states), BF),
+            V((half_t, num_states, num_states), BF),
+            V((half_t, num_states, num_states), BF),
+            V((blocks, half_t, rows, num_states), F32),
+            V((blocks, half_t, rows, num_states), F32),
+            V((blocks, rows, num_states), BF),
+            V((blocks, rows, num_states), BF),
+            V((half_t, 2, half, half), F32),
+            V((half_t, zr, half), F32),
+            V((4, 8, 128), F32),
+            V((zr, 128), F32),
+            V((zr, 128), F32),
+            D((nsrc,)), D((nsrc,)), D((2 * own_t,)), D((own_t,)),
+            D((blocks,)), D((blocks,)), D((2,)), D((2,)), D((3,)), D((3,)),
+        ],
+        compiler_params=pltpu.CompilerParams(
+            collective_id=0, has_side_effects=True, vmem_limit_bytes=56 * 1024 * 1024),
+        name="chain",
+    )(earnings.T, starts[None], lengths[None], block_count, trans_logits,
+      init_logits[None], state_mean[None], log_sd[None])
+    return grad, ll[0, 0:1]
+
+
 def solution(mesh):
+    fits = mesh.shape["per"] == 2 and mesh.shape["st"] == 2 and mesh.shape["hh"] == 4
+    body = fused_device if fits else per_device
     placed = (
         P(("hh", "per"), None),
         P(("hh", "per")),
@@ -168,7 +512,7 @@
         P("grp"),
     )
     return jax.shard_map(
-        per_device,
+        body,
         mesh=mesh,
         in_specs=placed,
         out_specs=(P(("grp", "per"), "hh", "st"), P("grp")),

time: 301 us -> 50.6 us (0.17)
  waiting for transfers between devices: 71.5 us -> 0 us
  matrix products: 63.4 us -> 0 us
  other arithmetic: 53.2 us -> 0 us
  Pallas kernels: 0 us -> 44.3 us
  local copies, waits for them, and re-layouts: 36.2 us -> 3.62 us
  blocking collectives: 24 us -> 0 us
  starting transfers between devices: 20 us -> 0 us
  between operations: 19 us -> 2.47 us
  loops' own time: 11.4 us -> 0 us
    dot_general x46 -> x0, matrix products: 63.4 us -> none  [the longest x16 25.6 us: forward(): jnp.dot(prev_alpha, matrix, precision=top_precision, preferred_element_ty...]
    reduce_scatter x2 -> x0, waiting for transfers between devices: 54.8 us -> none  [the longest x1 41.3 us: per_device(): lax.psum_scatter(partial_counts, 'hh', scatter_dimension=1, tiled=True)]
    pallas_call x0 -> x1, Pallas kernels: none -> 44.3 us  [fused_device(): pl.pallas_call(functools.partial(fused_kernel, cfg), out_shape=(jax.Shape...]
    psum x2 -> x0, blocking collectives: 24 us -> none  [the longest x1 21 us: per_device(): loglik_all, years_all = lax.psum((loglik_core, years_core), ('hh', 'per'))]
    select_n x35 -> x0, other arithmetic: 21.2 us -> none  [the longest x32 20.9 us: forward(): scale_now = jnp.where(seen_now, jnp.sum(joint_mass, axis=1), 1.0)]
    all_to_all x4 -> x0, starting transfers between devices: 19.9 us -> none  [the longest x1 7.28 us: per_device(): lax.all_to_all(count_out, ('hh', 'per'), split_axis=1, concat_axis=1, til...]
    dynamic_slice x31 -> x0, local copies, waits for them, and re-layouts: 18.2 us -> none  [the longest x16 9.38 us: per_device(): lax.scan(forward, start_alpha, (trans_probs, columns, period_ids))]
    all_to_all x4 -> x0, waiting for transfers between devices: 16 us -> none  [the longest x1 6.24 us: per_device(): lax.all_to_all(starts.reshape(source_rows, group_size), ('hh', 'per'), sp...]
  transfers between devices with their start and end apart: 7 -> 0, of which waited for: 5 -> 0; matrix products, arithmetic and copies ran while one was open for 5% -> 0% of each run, Pallas kernels for 0% -> 0%
where the time goes in v3:
time: 50.6 us; the launch traced here: 50.3 us
  Pallas kernels  44.3 us (88%)
  local copies, waits for them, and re-layouts  3.62 us (7%)
  between operations  2.47 us (5%)
    pallas_call x1, Pallas kernels, fused_device(): pl.pallas_call(functools.partial(fused_kernel, cfg), out_shape=(jax.Shape...  44.3 us
    unnamed x7, local copies, waits for them, and re-layouts  2.47 us

profile of v3, /device:TPU:0, one launch (start us, length us, event | category | flops | bytes accessed | tf_op | source)
XLA Modules:
  0.0 50.3 jit_solution(2244393048077403613)
XLA Ops:
  1.3 0.0 copy-start
  1.3 0.7 %copy-done = s32[384]{0:T(512)S(1)} copy-done((s32[384]{0:T(512)S(1)}, s32[384]{0:T(512)}, u32[]{:S(2)}) %copy-start) | copy-done | bytes 1560
  2.0 0.0 copy-start.1
  2.0 0.6 %broadcast_in_dim.15.begin = s32[1,384]{1,0:T(1,128)} reshape(s32[384]{0:T(512)S(1)} %copy-done) | data formatting | bytes 3072 | tf_op jit(solution)/shard_map/broadcast_in_dim | solution.py:496
  2.5 0.1 copy-done.1
  2.6 0.6 %broadcast_in_dim.16.length = s32[1,384]{1,0:T(1,128)} reshape(s32[384]{0:T(512)S(1)} %copy-done.1) | data formatting | bytes 3072 | tf_op jit(solution)/shard_map/broadcast_in_dim | solution.py:496
  3.2 44.3 %chain.1 = (f32[8,64,128]{2,1,0:T(8,128)}, f32[1,128]{1,0:T(1,128)}) custom-call(f32[16,384]{1,0:T(8,128)} %bitcast.6, s32[1,384]{1,0:T(1,128)} %broadcast_in_dim.15.begin, s32[1,384]{1,0:T(1,128)} %broadcast_in_dim.16.length, s32[1]{0:T(128)S(6)} %copy.12.count, bf16[4,256,256]{2,1,0:T(8,128)(2,1)} %logits.1, f32[1,256]{1,0:T(1,128)} %bitcast.7, ...), custom_call_target="tpu_custom_call" | custom-call | tf_op jit(solution)/shard_map/chain/pallas_call | solution.py:468
  47.5 0.0 copy-start.2
  47.5 1.7 %copy.13 = f32[8,64,128]{2,1,0:T(8,128)} copy(f32[8,64,128]{2,1,0:T(8,128)} %get-tuple-element.8) | data formatting | bytes 524288
  49.2 0.0 copy-done.2
Async XLA Ops:
  1.3 0.7 %copy-start = (s32[384]{0:T(512)S(1)}, s32[384]{0:T(512)}, u32[]{:S(2)}) copy-start(s32[384]{0:T(512)} %param.9) | copy-start | bytes 4612
  2.0 0.7 %copy-start.1 = (s32[384]{0:T(512)S(1)}, s32[384]{0:T(512)}, u32[]{:S(2)}) copy-start(s32[384]{0:T(512)} %param.10) | copy-start | bytes 4612
  47.5 1.7 %copy-start.2 = (f32[1,128]{1,0:T(1,128)S(1)}, f32[1,128]{1,0:T(1,128)}, u32[]{:S(2)}) copy-start(f32[1,128]{1,0:T(1,128)} %get-tuple-element.5) | copy-start | bytes 1540

commit v4 on v3

--- a/solution.py
+++ b/solution.py
@@ -192,7 +192,7 @@
                  pack, got, people, lg, phi, plo, amem, bmem, xsend, xrecv, cacc, crecv,
                  llbox, rts, rtr,
                  hs_sem, hr_sem, lr_sem, ls_sem, xs_sem, xr_sem, c_sem, r_sem, lls_sem, llr_sem):
-    nz, nt, half_t, own_t, rows, num_states, blocks = cfg
+    nz, nt, half_t, own_t, held, rows, num_states, blocks = cfg
     x = lax.axis_index("per")
     z = lax.axis_index("hh")
     s = lax.axis_index("st")
@@ -230,7 +230,7 @@
     cnt = count[0].astype(F32)
     spot = lax.broadcasted_iota(jnp.int32, (1, slots), 1).astype(F32)
     lens = length[...].astype(F32)
-    own_years = jnp.sum(jnp.where(spot < cnt * float(rows), lens, 0.0), axis=1, keepdims=True)
+    own_years = jnp.sum(jnp.where(spot < cnt * float(held), lens, 0.0), axis=1, keepdims=True)
     table = jnp.concatenate(
         [earn[...], begin[...].astype(F32), lens, jnp.full((1, slots), 1.0, F32) * cnt,
          jnp.broadcast_to(own_years, (1, slots)), jnp.zeros((4, slots), F32)], axis=0)
@@ -280,7 +280,7 @@
     years = jnp.zeros((1, 1), F32)
     bases, lives = [], []
     for src in range(nsrc):
-        live = got[src, nt + 2:nt + 3, 0:1] * float(rows // 2)
+        live = got[src, nt + 2:nt + 3, 0:1] * float(held // 2)
         years = years + got[src, nt + 3:nt + 4, 0:1]
         bases.append(base)
         lives.append(live)
@@ -310,13 +310,13 @@
         cacc[k, 1] += part[:, half:]
 
     def send_across(b, v):
-        xsend[b] = v.astype(BF)
+        xsend[b] = v
         rcopy(xsend.at[b], xrecv.at[b], xs_sem.at[b], xr_sem.at[b], across).start()
 
     def take_across(b):
         c = rcopy(xsend.at[b], xrecv.at[b], xs_sem.at[b], xr_sem.at[b], across)
         c.wait_recv()
-        return xrecv[b].astype(F32)
+        return xrecv[b]
 
     def chosen(v):
         return jnp.where(z // per_half == 0, v[:, :half], v[:, half:])
@@ -458,10 +458,10 @@
     half_t = nt // 2
     half = num_states // 2
     zr = num_states // nz
-    rows = HB
-    blocks = nsrc // 2
+    rows = HB * 2
+    blocks = nsrc // 4
     wide_slab = -(-(slot_rows // 2) // 128) * 128
-    cfg = (nz, nt, half_t, own_t, rows, num_states, blocks)
+    cfg = (nz, nt, half_t, own_t, HB, rows, num_states, blocks)
     V = pltpu.VMEM
     D = pltpu.SemaphoreType.DMA
     vm = pl.BlockSpec(memory_space=pltpu.VMEM)
@@ -480,8 +480,8 @@
             V((half_t, num_states, num_states), BF),
             V((blocks, half_t, rows, num_states), F32),
             V((blocks, half_t, rows, num_states), F32),
-            V((blocks, rows, num_states), BF),
-            V((blocks, rows, num_states), BF),
+            V((blocks, rows, num_states), F32),
+            V((blocks, rows, num_states), F32),
             V((half_t, 2, half, half), F32),
             V((half_t, zr, half), F32),
             V((4, 8, 128), F32),

time: 50.6 us -> 44.9 us (0.89)
  Pallas kernels: 44.3 us -> 38.5 us
    pallas_call x1, Pallas kernels: 44.3 us -> 38.5 us  [fused_device(): pl.pallas_call(functools.partial(fused_kernel, cfg), out_shape=(jax.Shape...]
where the time goes in v4:
time: 44.9 us; the launch traced here: 44.6 us
  Pallas kernels  38.5 us (86%)
  local copies, waits for them, and re-layouts  3.62 us (8%)
  between operations  2.47 us (6%)
    pallas_call x1, Pallas kernels, fused_device(): pl.pallas_call(functools.partial(fused_kernel, cfg), out_shape=(jax.Shape...  38.5 us
    unnamed x7, local copies, waits for them, and re-layouts  2.47 us

profile of v4, /device:TPU:0, one launch (start us, length us, event | category | flops | bytes accessed | tf_op | source)
XLA Modules:
  0.0 44.6 jit_solution(5741398181173539699)
XLA Ops:
  1.3 0.0 copy-start
  1.3 0.7 %copy-done = s32[384]{0:T(512)S(1)} copy-done((s32[384]{0:T(512)S(1)}, s32[384]{0:T(512)}, u32[]{:S(2)}) %copy-start) | copy-done | bytes 1560
  2.0 0.0 copy-start.1
  2.0 0.6 %broadcast_in_dim.15.begin = s32[1,384]{1,0:T(1,128)} reshape(s32[384]{0:T(512)S(1)} %copy-done) | data formatting | bytes 3072 | tf_op jit(solution)/shard_map/broadcast_in_dim | solution.py:496
  2.5 0.1 copy-done.1
  2.6 0.6 %broadcast_in_dim.16.length = s32[1,384]{1,0:T(1,128)} reshape(s32[384]{0:T(512)S(1)} %copy-done.1) | data formatting | bytes 3072 | tf_op jit(solution)/shard_map/broadcast_in_dim | solution.py:496
  3.2 38.5 %chain.1 = (f32[8,64,128]{2,1,0:T(8,128)}, f32[1,128]{1,0:T(1,128)}) custom-call(f32[16,384]{1,0:T(8,128)} %bitcast.6, s32[1,384]{1,0:T(1,128)} %broadcast_in_dim.15.begin, s32[1,384]{1,0:T(1,128)} %broadcast_in_dim.16.length, s32[1]{0:T(128)S(6)} %copy.12.count, bf16[4,256,256]{2,1,0:T(8,128)(2,1)} %logits.1, f32[1,256]{1,0:T(1,128)} %bitcast.7, ...), custom_call_target="tpu_custom_call" | custom-call | tf_op jit(solution)/shard_map/chain/pallas_call | solution.py:468
  41.8 0.0 copy-start.2
  41.8 1.7 %copy.13 = f32[8,64,128]{2,1,0:T(8,128)} copy(f32[8,64,128]{2,1,0:T(8,128)} %get-tuple-element.8) | data formatting | bytes 524288
  43.5 0.0 copy-done.2
Async XLA Ops:
  1.3 0.7 %copy-start = (s32[384]{0:T(512)S(1)}, s32[384]{0:T(512)}, u32[]{:S(2)}) copy-start(s32[384]{0:T(512)} %param.9) | copy-start | bytes 4612
  2.0 0.7 %copy-start.1 = (s32[384]{0:T(512)S(1)}, s32[384]{0:T(512)}, u32[]{:S(2)}) copy-start(s32[384]{0:T(512)} %param.10) | copy-start | bytes 4612
  41.8 1.7 %copy-start.2 = (f32[1,128]{1,0:T(1,128)S(1)}, f32[1,128]{1,0:T(1,128)}, u32[]{:S(2)}) copy-start(f32[1,128]{1,0:T(1,128)} %get-tuple-element.5) | copy-start | bytes 1540
